TPU v7x, 512 devices: a whole 4x4x16 slice. The times are simulated.
512 devices in a mesh: row: 16 (over z_lo, x), col: 32 (over y, z_hi, core).
Axes of the slice: x: 4, y: 4, z: 16 (z_hi: 4, z_lo: 4; z = z_hi * 4 + z_lo), core: 2. Of those that a mesh axis runs over, the one named last changes fastest.
Arguments:
- alignment: int32 [512, 480], P(None, 'row'), may hold values from 0 to 20
- seq_weight: float32 [512], replicated, may hold values from 0.1 to 1
- couplings: float32 [10080, 10080], P('row', 'col'), may hold values from -0.15 to 0.15, as said below
- pair_mean: float32 [10080, 10080], P('row', 'col'), may hold values from -4 to 4, as said below
- pair_square: float32 [10080, 10080], P('row', 'col'), may hold values from 1 to 100, as said below
- fields: float32 [10080], P('row'), may hold values from -2 to 2
- field_mean: float32 [10080], P('row'), may hold values from -4 to 4
- field_square: float32 [10080], P('row'), may hold values from 1 to 100
Outputs:
- updated_pairs: float32 [10080, 10080], P('row', 'col')
- updated_pair_mean: float32 [10080, 10080], P('row', 'col')
- updated_pair_square: float32 [10080, 10080], P('row', 'col')
- updated_fields: float32 [10080], P('row')
- updated_field_mean: float32 [10080], P('row')
- updated_field_square: float32 [10080], P('row')
Inputs may be any that keep to these rules, and one draw needn't show every extreme that they name: alignment holds whole numbers below 21; a program may send them packed, several to one 32-bit word. couplings is symmetric (entry (k, m) equals entry (m, k)); entries whose row and column belong to the same residue (k // 21 == m // 21) are zero. pair_mean is symmetric; entries whose row and column belong to the same residue are zero. pair_square is symmetric.
All inputs are finite; a program needn't handle non-finite values.
Results may differ from a plain program's by a relative error of at most 0.00005.
Values sent between devices are 32-bit elements; how exact they have to be, the bound alone decides.
A program may use at most 64 MiB of HBM per device.

v0:
```python
import jax
import jax.numpy as jnp
from jax import lax
from jax.sharding import Mesh
from jax.sharding import PartitionSpec as P

L = 480
Q = 21
COL = ("col_0", "col_1", "col_2")


def from_root(x, axis, root):
    return lax.dynamic_index_in_dim(lax.all_gather(x, axis), root, 0, keepdims=False)


def padded_to(lines, size):
    spare = -lines.shape[0] % size
    if not spare:
        return lines
    return jnp.concatenate([lines, jnp.zeros((spare, *lines.shape[1:]), lines.dtype)])


def copy_for_each(x, axis):
    copies = jnp.broadcast_to(x, (lax.axis_size(axis), *x.shape))
    return lax.all_to_all(copies, axis, split_axis=0, concat_axis=0, tiled=True)


def laid_out(blocks, dim):
    dims = list(blocks.shape[1:])
    dims[dim] *= blocks.shape[0]
    return jnp.moveaxis(blocks, 0, dim).reshape(dims)


def gathered_by_axis(x, axes, dim):
    far, near = axes
    leading = copy_for_each(x, far)
    blocks = jnp.swapaxes(copy_for_each(leading, near), 0, 1)
    return laid_out(blocks.reshape(-1, *x.shape), dim)


def in_blocks(x, dim, size):
    dims = x.shape
    blocks = x.reshape(*dims[:dim], size, dims[dim] // size, *dims[dim + 1 :])
    return jnp.moveaxis(blocks, dim, 0)


def sum_at_owner(x, axis, dim):
    blocks = in_blocks(x, dim, lax.axis_size(axis))
    arrived = lax.all_to_all(blocks, axis, split_axis=0, concat_axis=0, tiled=True)
    return arrived.sum(axis=0)


def summed_rows(x, axes, dim):
    far, near = axes
    blocks = in_blocks(x, dim, lax.axis_size(far))
    nearer = sum_at_owner(blocks, near, dim + 1)
    arrived = lax.all_to_all(nearer, far, split_axis=0, concat_axis=0, tiled=True)
    return arrived.sum(axis=0)


def nested_sum(x, axes):
    lines = x.reshape(-1, x.shape[-1])
    padded = padded_to(lines, lax.axis_size(axes[0]) * lax.axis_size(axes[1]))
    whole = gathered_by_axis(summed_rows(padded, axes, 0), axes, 0)
    return lax.slice_in_dim(whole, 0, len(lines)).reshape(x.shape)


def collect(x, axis, dim):
    blocks = copy_for_each(x, axis)
    return laid_out(blocks, dim)


def nested_sum_2(x, axes):
    lines = x.reshape(-1, x.shape[-1])
    padded = padded_to(lines, lax.axis_size(axes))
    whole = collect(sum_at_owner(padded, axes, 0), axes, 0)
    return lax.slice_in_dim(whole, 0, len(lines)).reshape(x.shape)


def encode_states(states):
    levels = lax.broadcasted_iota(jnp.int32, (1, 1, Q), 2)
    encoded = (states[:, :, None] == levels).astype(jnp.float32)
    return encoded.reshape(states.shape[0], states.shape[1] * Q)


def residue_totals(values):
    width = values.shape[1]
    member_rows = lax.broadcasted_iota(jnp.int32, (width, width // Q), 0) // Q
    member_cols = lax.broadcasted_iota(jnp.int32, (width, width // Q), 1)
    member = (member_rows == member_cols).astype(jnp.float32)
    totals = jnp.dot(
        values, member, precision=lax.Precision.HIGHEST, preferred_element_type=jnp.float32
    )
    return jnp.dot(
        totals, member.T, precision=lax.Precision.HIGHEST, preferred_element_type=jnp.float32
    )


def residuals(energy, encoded, weights):
    powers = jnp.exp(energy)
    return weights[:, None] * (powers / residue_totals(powers) - encoded)


def adam_update(values, first_moment, second_moment, gradient):
    first_new = 0.9 * first_moment + 0.1 * gradient
    second_new = 0.999 * second_moment + 0.001 * gradient * gradient
    change = (
        0.05 * (first_new / (1.0 - 0.9**10)) / (jnp.sqrt(second_new / (1.0 - 0.999**10)) + 1e-08)
    )
    return (values - change, first_new, second_new)


def on_device(
    alignment, seq_weight, couplings, pair_mean, pair_square, fields, field_mean, field_square
):
    row_residues = alignment.shape[1]
    column_width = couplings.shape[1]
    column_residues = column_width // Q
    per_owner = row_residues // column_residues
    column_index = lax.axis_index(COL)
    row_index = lax.axis_index("row")
    owner_row = column_index // per_owner
    offset = column_index % per_owner * column_residues
    own_states = lax.dynamic_slice_in_dim(alignment, offset, column_residues, 1)
    column_states = from_root(own_states, "row", owner_row)
    column_onehot = encode_states(column_states)
    row_onehot = encode_states(alignment)
    partial_value = lax.dot_general(
        column_onehot,
        couplings,
        (((1,), (1,)), ((), ())),
        precision=lax.Precision.HIGHEST,
        preferred_element_type=jnp.float32,
    )
    energy = nested_sum(partial_value, (("col_0", "col_1"), "col_2")) + fields[None, :]
    weighted = residuals(energy, row_onehot, seq_weight)
    contract = (((0,), (0,)), ((), ()))
    half_rows = lax.dot_general(
        weighted,
        column_onehot,
        contract,
        precision=lax.Precision.HIGHEST,
        preferred_element_type=jnp.float32,
    )
    field_slice = lax.dynamic_slice_in_dim(fields, offset * Q, column_width, 0)
    on_owner = (row_index == owner_row).astype(jnp.float32)
    column_partial = (
        jnp.dot(
            row_onehot,
            couplings,
            precision=lax.Precision.HIGHEST,
            preferred_element_type=jnp.float32,
        )
        + on_owner * field_slice[None, :]
    )
    column_energy = nested_sum_2(column_partial, "row")
    column_weighted = residuals(column_energy, column_onehot, seq_weight)
    half_columns = lax.dot_general(
        row_onehot,
        column_weighted,
        contract,
        precision=lax.Precision.HIGHEST,
        preferred_element_type=jnp.float32,
    )
    row_ids = (
        row_index * row_residues + lax.broadcasted_iota(jnp.int32, (couplings.shape[0], 1), 0) // Q
    )
    column_ids = (
        column_index * column_residues + lax.broadcasted_iota(jnp.int32, (1, column_width), 1) // Q
    )
    off_diagonal = row_ids != column_ids
    pair_grad = jnp.where(off_diagonal, half_rows + half_columns, 0.0) + 0.2 * (L - 1) * couplings
    field_grad = jnp.sum(weighted, axis=0)
    new_pairs, new_pair_mean, new_pair_square = adam_update(
        couplings, pair_mean, pair_square, pair_grad
    )
    new_fields, new_field_mean, new_field_square = adam_update(
        fields, field_mean, field_square, field_grad
    )
    return (new_pairs, new_pair_mean, new_pair_square, new_fields, new_field_mean, new_field_square)


def solution(mesh):
    finer = Mesh(
        mesh.devices.reshape(mesh.shape["row"], 4, 4, 2), ("row", "col_0", "col_1", "col_2")
    )
    in_specs = (
        P(None, "row"),
        P(),
        P("row", COL),
        P("row", COL),
        P("row", COL),
        P("row"),
        P("row"),
        P("row"),
    )
    out_specs = (P("row", COL), P("row", COL), P("row", COL), P("row"), P("row"), P("row"))
    return jax.shard_map(
        on_device, mesh=finer, in_specs=in_specs, out_specs=out_specs, check_vma=False
    )
```

profile of v0, /device:TPU:1, one launch (start us, length us, event | category | flops | bytes accessed | tf_op | source)
XLA Modules:
  0.0 221.0 jit_solution(6049478343303411736)
XLA Ops:
  0.7 0.8 constant_dynamic-slice_fusion.1
  1.5 39.9 %all-gather = s32[8192,15]{0,1:T(8,128)S(1)} all-gather(s32[512,15]{0,1:T(8,128)S(1)} %constant_dynamic-slice_fusion.1), channel_id=2, replica_groups=mesh['row'=16,'col_0'=4,'col_1'=4,'col_2'=2] {'row'}, dimensions={0}, use_global_device_ids=true | all-gather | bytes 522240 | tf_op jit(solution)/shard_map/all_gather | solution.py:13
  41.4 0.3 copy.37
  41.8 0.1 copy.36
  41.9 4.5 %eq.71.clone = s32[512,15,21]{2,1,0:T(8,128)} broadcast(s32[512,15]{1,0:T(8,128)S(1)} %bitcast.40), dimensions={0,1} | broadcast | bytes 675840 | tf_op jit(solution)/shard_map/eq | solution.py:82
  46.5 3.7 %eq.72 = s32[16,2,16,315]{3,2,1,0:T(8,128)S(1)} reshape(s32[512,15,21]{2,1,0:T(8,128)} %eq.71.clone) | data formatting | bytes 1290240 | tf_op jit(solution)/shard_map/eq | solution.py:82
  50.2 0.1 eq.74
  50.3 0.0 copy-done.1
  50.3 1.3 convolution_bitcast_fusion
  51.7 0.1 copy.28
  51.7 12.5 %all_to_all.30 = f32[2,16,16,630]{3,2,1,0:T(8,128)S(1)} all-to-all(f32[2,16,16,630]{3,2,1,0:T(8,128)S(1)} %copy.28), channel_id=1, replica_groups=mesh['row'=16,'col_0'=4,'col_1'=4,'col_2'=2] {'col_2'}, dimensions={0} | all-to-all | bytes 2580480 | tf_op jit(solution)/shard_map/all_to_all | solution.py:49
  64.3 1.0 reduce_sum.36
  65.3 15.0 %all-to-all-start.1 = ((f32[16,16,630]{2,1,0:T(8,128)}), f32[16,16,630]{2,1,0:T(8,128)S(1)}, u32[]{:S(2)}, u32[]{:S(2)}) async-start(f32[16,16,630]{2,1,0:T(8,128)} %reduce_sum.36), calls=%async_computation.1 | async-start | bytes 1310720 | tf_op jit(solution)/shard_map/all_to_all | solution.py:57
  80.2 0.2 eq.78
  80.4 0.0 copy-start.9
  80.4 0.2 eq.79
  80.6 0.0 copy-start.2
  80.6 0.1 eq.81
  80.7 0.4 copy-done.9
  81.1 0.1 dynamic-slice_multiply_fusion
  81.2 0.2 broadcast_compare_fusion
  81.4 0.0 copy-start.6
  81.4 0.7 copy-done.6
  82.2 1.0 convolution_add_fusion.1
  83.2 1.1 copy.31
  84.3 28.5 %all-to-all-done.1 = f32[16,16,630]{2,1,0:T(8,128)S(1)} async-done(((f32[16,16,630]{2,1,0:T(8,128)}), f32[16,16,630]{2,1,0:T(8,128)S(1)}, u32[]{:S(2)}, u32[]{:S(2)}) %all-to-all-start.1) | async-done | bytes 645152 | tf_op jit(solution)/shard_map/all_to_all | solution.py:57
  112.8 3.6 %all-to-all-start.4 = ((f32[16,32,315]{2,1,0:T(8,128)}), f32[16,32,315]{2,1,0:T(8,128)S(1)}, u32[]{:S(2)}, u32[]{:S(2)}) async-start(f32[16,32,315]{2,1,0:T(8,128)} %bitcast.5), calls=%async_computation.4 | async-start | bytes 1572864 | tf_op jit(solution)/shard_map/all_to_all | solution.py:49
  116.5 18.4 %all-to-all-done.4 = f32[16,32,315]{2,1,0:T(8,128)S(1)} async-done(((f32[16,32,315]{2,1,0:T(8,128)}), f32[16,32,315]{2,1,0:T(8,128)S(1)}, u32[]{:S(2)}, u32[]{:S(2)}) %all-to-all-start.4) | async-done | bytes 645152 | tf_op jit(solution)/shard_map/all_to_all | solution.py:49
  134.9 0.9 broadcast_in_dim.9
  135.8 6.0 %all-to-all-start.2 = ((f32[16,16,630]{2,1,0:T(8,128)}), f32[16,16,630]{2,1,0:T(8,128)S(1)}, u32[]{:S(2)}, u32[]{:S(2)}) async-start(f32[16,16,630]{2,1,0:T(8,128)} %broadcast_in_dim.9), calls=%async_computation.2 | async-start | bytes 1310720 | tf_op jit(solution)/shard_map/all_to_all | solution.py:25
  141.8 0.1 reduce_sum.38
  141.9 23.9 %all-to-all-done.2 = f32[16,16,630]{2,1,0:T(8,128)S(1)} async-done(((f32[16,16,630]{2,1,0:T(8,128)}), f32[16,16,630]{2,1,0:T(8,128)S(1)}, u32[]{:S(2)}, u32[]{:S(2)}) %all-to-all-start.2) | async-done | bytes 645152 | tf_op jit(solution)/shard_map/all_to_all | solution.py:25
  165.8 0.1 broadcast_in_dim.20
  165.8 6.7 %all_to_all.31 = f32[2,16,16,630]{3,2,1,0:T(8,128)S(1)} all-to-all(f32[2,16,16,630]{3,2,1,0:T(8,128)S(1)} %broadcast_in_dim.20), channel_id=1, replica_groups=mesh['row'=16,'col_0'=4,'col_1'=4,'col_2'=2] {'col_2'}, dimensions={0} | all-to-all | bytes 2580480 | tf_op jit(solution)/shard_map/all_to_all | solution.py:25
  172.5 1.0 broadcast_in_dim.21
  173.5 19.4 %all-to-all-start.5 = ((f32[16,32,315]{2,1,0:T(8,128)}), f32[16,32,315]{2,1,0:T(8,128)S(1)}, u32[]{:S(2)}, u32[]{:S(2)}) async-start(f32[16,32,315]{2,1,0:T(8,128)} %broadcast_in_dim.21), calls=%async_computation.5 | async-start | bytes 1572864 | tf_op jit(solution)/shard_map/all_to_all | solution.py:25
  192.9 0.1 eq.71
  193.0 0.1 eq.84
  193.2 0.8 broadcast_compare_fusion.1
  194.0 0.1 copy.29
  194.1 1.5 copy.30
  195.6 15.7 %all-to-all-done.5 = f32[16,32,315]{2,1,0:T(8,128)S(1)} async-done(((f32[16,32,315]{2,1,0:T(8,128)}), f32[16,32,315]{2,1,0:T(8,128)S(1)}, u32[]{:S(2)}, u32[]{:S(2)}) %all-to-all-start.5) | async-done | bytes 645152 | tf_op jit(solution)/shard_map/all_to_all | solution.py:25
  211.3 0.1 exp.10
  211.4 0.0 copy-start.14
  211.4 1.1 copy.32
  212.5 0.9 fusion.6
  213.4 0.0 copy-done.14
  213.4 0.1 copy-done.7
  213.5 1.2 fusion.34
  214.7 0.0 copy-start.5
  214.7 1.1 fusion.35
  215.8 0.6 fusion.12
  216.4 0.0 copy-start.10
  216.4 0.0 copy-start.11
  216.4 0.0 copy-start.3
  216.4 0.0 copy-start.12
  216.4 0.0 copy-start.13
  216.4 0.6 fusion.5
  217.0 0.0 copy-done.10
  217.1 0.0 copy-done.11
  217.1 0.6 divide_subtract_fusion.1
  217.7 0.1 copy-done.12
  217.8 0.3 copy-done.13
  218.1 2.9 %divide_subtract_fusion = (f32[630,315]{0,1:T(8,128)}, f32[630,315]{0,1:T(8,128)}, f32[630,315]{0,1:T(8,128)}) fusion(f32[630,315]{0,1:T(8,128)S(1)} %copy-done.3, f32[630,315]{0,1:T(8,128)S(1)} %copy-done.12, f32[630,315]{0,1:T(8,128)S(1)} %copy-done.13, f32[630,315]{0,1:T(8,128)S(1)} %fusion.35, pred[512,630]{0,1:T(8,128)(4,1)S(1)} %copy-done.7, ...), kind=kOutput, calls=%fused_computation.16 | convolution fusion | flops 1222650368 | bytes 6528060 | tf_op jit(solution)/shard_map/dot_general | solution.py:158
  (24 shorter events, 0.2 us)
Async XLA Ops:
  46.5 3.8 %copy-start.1 = (f32[630,315]{0,1:T(8,128)S(1)}, f32[630,315]{0,1:T(8,128)}, u32[]{:S(2)}) copy-start(f32[630,315]{0,1:T(8,128)} %param.10) | copy-start | bytes 2381404
  64.3 16.0 %copy-start.8 = (s32[512,30]{0,1:T(8,128)S(1)}, s32[512,30]{0,1:T(8,128)}, u32[]{:S(2)}) copy-start(s32[512,30]{0,1:T(8,128)} %param.8) | copy-start | bytes 184324
  65.3 47.6 %all-to-all-start.1 = ((f32[16,16,630]{2,1,0:T(8,128)}), f32[16,16,630]{2,1,0:T(8,128)S(1)}, u32[]{:S(2)}, u32[]{:S(2)}) async-start(f32[16,16,630]{2,1,0:T(8,128)} %reduce_sum.36), calls=%async_computation.1 | async-start | bytes 1310720 | tf_op jit(solution)/shard_map/all_to_all | solution.py:57
  80.4 0.7 copy-start.9
  80.6 1.6 copy-start.2
  81.4 0.7 copy-start.6
  112.8 22.1 %all-to-all-start.4 = ((f32[16,32,315]{2,1,0:T(8,128)}), f32[16,32,315]{2,1,0:T(8,128)S(1)}, u32[]{:S(2)}, u32[]{:S(2)}) async-start(f32[16,32,315]{2,1,0:T(8,128)} %bitcast.5), calls=%async_computation.4 | async-start | bytes 1572864 | tf_op jit(solution)/shard_map/all_to_all | solution.py:49
  135.8 30.0 %all-to-all-start.2 = ((f32[16,16,630]{2,1,0:T(8,128)}), f32[16,16,630]{2,1,0:T(8,128)S(1)}, u32[]{:S(2)}, u32[]{:S(2)}) async-start(f32[16,16,630]{2,1,0:T(8,128)} %broadcast_in_dim.9), calls=%async_computation.2 | async-start | bytes 1310720 | tf_op jit(solution)/shard_map/all_to_all | solution.py:25
  173.5 37.9 %all-to-all-start.5 = ((f32[16,32,315]{2,1,0:T(8,128)}), f32[16,32,315]{2,1,0:T(8,128)S(1)}, u32[]{:S(2)}, u32[]{:S(2)}) async-start(f32[16,32,315]{2,1,0:T(8,128)} %broadcast_in_dim.21), calls=%async_computation.5 | async-start | bytes 1572864 | tf_op jit(solution)/shard_map/all_to_all | solution.py:25
  195.6 16.9 %copy-start = (f32[512,630]{0,1:T(8,128)S(1)}, f32[512,630]{0,1:T(8,128)}, u32[]{:S(2)}) copy-start(f32[512,630]{0,1:T(8,128)} %copy.30) | copy-start | bytes 3870724
  211.4 2.0 copy-start.14
  212.5 1.0 copy-start.7
  213.5 1.2 copy-start.4
  214.7 1.7 copy-start.5
  216.4 0.7 copy-start.10
  216.4 0.7 copy-start.11
  216.4 1.3 copy-start.3
  216.4 1.4 copy-start.12
  216.4 1.6 copy-start.13
where the time goes:
time: 223 us; the launch traced here: 221 us
  waiting for transfers between devices  86.5 us (39%)
  blocking collectives  59 us (26%)
  starting transfers between devices  44 us (20%)
  local copies, waits for them, and re-layouts  17.9 us (8%)
  matrix products  9.56 us (4%)
  other arithmetic  2.92 us (1%)
    all_gather x1, blocking collectives, from_root(): lax.all_gather(x, axis)  39.9 us
    all_to_all x2, waiting for transfers between devices, copy_for_each(): return lax.all_to_all(copies, axis, split_axis=0, concat_axis=0, tiled=True)  39.5 us
    all_to_all x1, waiting for transfers between devices, summed_rows(): lax.all_to_all(nearer, far, split_axis=0, concat_axis=0, tiled=True)  28.5 us
    all_to_all x2, starting transfers between devices, copy_for_each(): return lax.all_to_all(copies, axis, split_axis=0, concat_axis=0, tiled=True)  25.5 us
    all_to_all x1, waiting for transfers between devices, sum_at_owner(): lax.all_to_all(blocks, axis, split_axis=0, concat_axis=0, tiled=True)  18.4 us
    all_to_all x1, starting transfers between devices, summed_rows(): lax.all_to_all(nearer, far, split_axis=0, concat_axis=0, tiled=True)  15 us
    all_to_all x1, blocking collectives, sum_at_owner(): lax.all_to_all(blocks, axis, split_axis=0, concat_axis=0, tiled=True)  12.5 us
    eq x10, local copies, waits for them, and re-layouts, encode_states(): encoded = (states[:, :, None] == levels).astype(jnp.float32)  8.96 us
  transfers between devices with their start and end apart: 4, of which 4 were waited for; matrix products, arithmetic and copies ran while one was open for 3% of the time, Pallas kernels for 0%

commit v1 on v0

v1 whole, which is shorter than its diff:
```python
import jax
import jax.numpy as jnp
from jax import lax
from jax.experimental import pallas as pl
from jax.experimental.pallas import tpu as pltpu
from jax.sharding import PartitionSpec as P

L = 480
Q = 21
MESH = pl.DeviceIdType.MESH
F32 = jnp.float32
BF16 = jnp.bfloat16


def two_parts(x):
    high = x.astype(BF16)
    return high, (x - high.astype(F32)).astype(BF16)


def three_parts(x):
    high = x.astype(BF16)
    rest = x - high.astype(F32)
    mid = rest.astype(BF16)
    return high, mid, (rest - mid.astype(F32)).astype(BF16)


def dot(a, b, dims=((1,), (0,))):
    return lax.dot_general(a, b, (dims, ((), ())), preferred_element_type=F32)


def residue_of(lane):
    return ((lane.astype(F32) + 0.5) * (1.0 / Q)).astype(jnp.int32)


def flip(i):
    return i + 1 - 2 * (i % 2)


def mirror(i):
    return 3 - i


def packed_column(lane):
    main = jnp.where(lane < 256, lane, lane - 256)
    tail = jnp.where(lane < 576, lane - 512, lane - 576)
    column = jnp.where(lane < 512, main, tail + 256)
    second = ((lane >= 256) & (lane < 512)) | (lane >= 576)
    return column, second, (lane < 512) | (tail < 59)


def kernel(
    al_ref, w_ref, j_ref, f_ref, g_ref, fg_ref,
    states, oc32, or32, j_high, j_low, part, got, xr, xc,
    r_in1, r_in2, r_in3, r_in4, c_in1, c_in2, c_in3, c_in4, wr, wc, acc,
    fpad, state_send, send, recv,
):
    row, col = lax.axis_index("row"), lax.axis_index("col")
    z_lo, x = row // 4, row % 4
    y, z_hi, core = col // 8, (col // 2) % 4, col % 2
    owner = col // 2

    def at_row(a, b):
        return (row, a * 8 + b * 2 + core)

    def at_col(a, b):
        return (b * 4 + a, col)

    partner = (row, y * 8 + z_hi * 2 + 1 - core)

    barrier = pltpu.get_barrier_semaphore()
    greeted = [at_row(flip(y), z_hi), at_row(mirror(y), z_hi), at_row(y, flip(z_hi))]
    greeted += [at_row(y, mirror(z_hi)), partner]
    greeted += [((row + d) % 16, col) for d in range(1, 16)]
    for device in greeted:
        pl.semaphore_signal(barrier, inc=1, device_id=device, device_id_type=MESH)

    fpad[...] = jnp.zeros_like(fpad)
    fpad[0:1, 0:630] = f_ref[...]
    alignment = al_ref[...].astype(F32).astype(BF16)
    pick_row = lax.broadcasted_iota(jnp.int32, (16, 30), 0)
    pick_col = lax.broadcasted_iota(jnp.int32, (16, 30), 1)
    pick = (pick_col == pick_row + 15 * core) & (pick_row < 15)
    own_states = dot(pick.astype(F32).astype(BF16), alignment, ((1,), (1,)))

    pl.semaphore_wait(barrier, len(greeted))

    state_copies = [
        pltpu.make_async_remote_copy(
            states, states, state_send.at[d], recv.at[0],
            device_id=((row + d) % 16, col), device_id_type=MESH,
        )
        for d in range(1, 16)
    ]

    @pl.when(row == owner)
    def _():
        states[...] = own_states
        fields = fpad[...]
        moved = jnp.where(core == 0, fields, pltpu.roll(fields, 325, 1))
        field_lane = lax.broadcasted_iota(jnp.int32, (1, 512), 1)
        states[15:16, :] = jnp.where(field_lane < 315, moved[0:1, 0:512], 0.0)
        for copy in state_copies:
            copy.start()

    copies = []

    def exchange(src, dst, device):
        at = len(copies) + 1
        copy = pltpu.make_async_remote_copy(
            src, dst, send.at[at], recv.at[at], device_id=device, device_id_type=MESH
        )
        copy.start()
        copies.append(copy)
        return copy

    j_high[...] = jnp.zeros_like(j_high)
    j_low[...] = jnp.zeros_like(j_low)
    high, low = two_parts(j_ref[...])
    j_high[0:630, 0:315] = high
    j_low[0:630, 0:315] = low

    lane_r = lax.broadcasted_iota(jnp.int32, (1, 640), 1)
    res_r = residue_of(lane_r)
    spread_r = lax.broadcasted_iota(jnp.int32, (30, 640), 0) == residue_of(
        lax.broadcasted_iota(jnp.int32, (30, 640), 1)
    )
    value_r = dot(alignment, spread_r.astype(F32).astype(BF16))
    hot_r = (value_r == (lane_r - res_r * Q).astype(F32)) & (lane_r < 630)
    hot_r = hot_r.astype(F32)
    or32[...] = hot_r.reshape(64, 8, 640)
    hot_r = hot_r.astype(BF16)

    top, bottom = hot_r[0:256], hot_r[256:512]
    tail_high, tail_low = j_high[:, 256:384], j_low[:, 256:384]
    tail_high2 = pltpu.roll(tail_high.astype(F32), 64, 1).astype(BF16)
    tail_low2 = pltpu.roll(tail_low.astype(F32), 64, 1).astype(BF16)
    main_high, main_low = j_high[:, 0:256], j_low[:, 0:256]
    xc[:, :, :, :, 0:256] = (dot(top, main_high) + dot(top, main_low)).reshape(4, 2, 4, 8, 256)
    xc[:, :, :, :, 256:512] = (dot(bottom, main_high) + dot(bottom, main_low)).reshape(4, 2, 4, 8, 256)
    xc[:, :, :, :, 512:640] = (
        dot(top, tail_high) + dot(top, tail_low) + dot(bottom, tail_high2) + dot(bottom, tail_low2)
    ).reshape(4, 2, 4, 8, 128)

    def order(i, half):
        first, second = flip(i), mirror(i)
        return (first, second) if half == 0 else (second, first)

    far = lambda i: (i + 2) % 4

    class Reduce:
        def __init__(self, a, b, at, total, in1, in2, in3, in4, full):
            self.a, self.b, self.at, self.total, self.full = a, b, at, total, full
            self.ins = (in1, in2, in3, in4)

        def step1(self):
            self.s1 = []
            for h in range(2):
                p, _ = order(self.a, h)
                to = self.at(p, self.b)
                self.s1.append([
                    exchange(self.total.at[p, h], self.ins[0].at[h, 0], to),
                    exchange(self.total.at[far(self.a), h], self.ins[0].at[h, 1], to),
                ])

        def step2(self):
            self.s2 = []
            for h in range(2):
                p, q = order(self.a, h)
                self.s1[h][1].wait_recv()
                self.total[q, h] += self.ins[0][h, 1]
                self.s2.append(exchange(self.total.at[q, h], self.ins[1].at[h], self.at(q, self.b)))
            for h in range(2):
                self.s1[h][0].wait_recv()
                self.total[self.a, h] += self.ins[0][h, 0]

        def step3(self):
            self.s3 = []
            for h in range(2):
                p, _ = order(self.b, h)
                self.s2[h].wait_recv()
                self.total[self.a, h] += self.ins[1][h]
                to = self.at(self.a, p)
                self.s3.append([
                    exchange(self.total.at[self.a, h, p], self.ins[2].at[h, 0], to),
                    exchange(self.total.at[self.a, h, far(self.b)], self.ins[2].at[h, 1], to),
                ])

        def step4(self):
            self.s4 = []
            for h in range(2):
                p, q = order(self.b, h)
                self.s3[h][1].wait_recv()
                self.total[self.a, h, q] += self.ins[2][h, 1]
                self.s4.append(
                    exchange(self.total.at[self.a, h, q], self.ins[3].at[h], self.at(self.a, q))
                )
            for h in range(2):
                self.s3[h][0].wait_recv()
                self.total[self.a, h, self.b] += self.ins[2][h, 0]

        def result(self):
            parts = []
            for h in range(2):
                self.s4[h].wait_recv()
                parts.append(self.total[self.a, h, self.b] + self.ins[3][h])
            return jnp.concatenate(parts, axis=0)

        def gather1(self, value):
            self.g1 = []
            for h in range(2):
                self.full[self.a, h, self.b] = value[8 * h : 8 * h + 8]
                _, q = order(self.b, h)
                own = self.full.at[self.a, h, self.b]
                self.g1.append(exchange(own, own, self.at(self.a, q)))

        def gather2(self):
            self.g2 = []
            for h in range(2):
                p, q = order(self.b, h)
                to = self.at(self.a, p)
                own, second = self.full.at[self.a, h, self.b], self.full.at[self.a, h, q]
                sent = [exchange(own, own, to)]
                self.g1[h].wait_recv()
                sent.append(exchange(second, second, to))
                self.g2.append(sent)

        def gather3(self):
            self.g3 = []
            for h in range(2):
                _, q = order(self.a, h)
                for copy in self.g2[h]:
                    copy.wait_recv()
                own = self.full.at[self.a, h]
                self.g3.append(exchange(own, own, self.at(q, self.b)))

        def gather4(self):
            self.g4 = []
            for h in range(2):
                p, q = order(self.a, h)
                to = self.at(p, self.b)
                own, second = self.full.at[self.a, h], self.full.at[q, h]
                sent = [exchange(own, own, to)]
                self.g3[h].wait_recv()
                sent.append(exchange(second, second, to))
                self.g4.append(sent)

        def gathered(self):
            for sent in self.g4:
                for copy in sent:
                    copy.wait_recv()

    cols = Reduce(x, z_lo, at_col, xc, c_in1, c_in2, c_in3, c_in4, wc)
    mine = wr.at[core]
    rows = Reduce(y, z_hi, at_row, xr, r_in1, r_in2, r_in3, r_in4, mine)
    cols.step1()

    @pl.when(row != owner)
    def _():
        state_copies[0].wait_recv()

    lane_c = lax.broadcasted_iota(jnp.int32, (1, 384), 1)
    spread_c = lax.broadcasted_iota(jnp.int32, (16, 384), 0) == residue_of(
        lax.broadcasted_iota(jnp.int32, (16, 384), 1)
    )
    state_rows = lax.broadcasted_iota(jnp.int32, (16, 512), 0)
    state_values = jnp.where(state_rows < 15, states[...], 0.0).astype(BF16)
    value_c = dot(state_values, spread_c.astype(F32).astype(BF16), ((0,), (0,)))
    hot_c = (value_c == (lane_c - residue_of(lane_c) * Q).astype(F32)) & (lane_c < 315)
    hot_c = hot_c.astype(F32)
    oc32[...] = hot_c.reshape(64, 8, 384)

    def row_part(which):
        lines = oc32[pl.ds(which * 32, 32)].reshape(256, 384).astype(BF16)
        sums = dot(lines, j_high[...], ((1,), (1,))) + dot(lines, j_low[...], ((1,), (1,)))
        return sums.reshape(4, 2, 4, 8, 640)

    part[...] = row_part(1 - core)
    across = exchange(part, got, partner)
    xr[...] = row_part(core)
    across.wait_recv()
    xr[...] += got[...]
    rows.step1()
    cols.step2()
    rows.step2()
    cols.step3()
    cols.step4()
    rows.step3()

    def line_weights(first):
        at = lax.broadcasted_iota(jnp.int32, (16, 512), 0)
        lane = lax.broadcasted_iota(jnp.int32, (16, 512), 1)
        at = jnp.where(at < 8, at, at + 24) + first
        return jnp.sum(jnp.where(lane == at, w_ref[...], 0.0), axis=1, keepdims=True)

    def residual(energy, hot, residue, weight):
        member = lax.broadcasted_iota(jnp.int32, (128, 640), 0) == residue
        member = member.astype(F32).astype(BF16)
        powers = jnp.exp(energy)
        lines = energy.shape[0]
        parts = dot(jnp.concatenate(three_parts(powers), axis=0), member, ((1,), (1,)))
        sums = parts[0:lines] + parts[lines : 2 * lines] + parts[2 * lines :]
        inverse = jnp.where(sums > 0.0, 1.0 / sums, 0.0)
        parts = dot(jnp.concatenate(three_parts(inverse), axis=0), member)
        inverse = parts[0:lines] + parts[lines : 2 * lines] + parts[2 * lines :]
        return weight * (powers * inverse - hot)

    energy = cols.result()
    column, second, valid = packed_column(lane_r)
    residue_c = jnp.where(valid, residue_of(column) + jnp.where(second, 32, 0), -1)
    first = x * 64 + z_lo * 8

    def column_lines(start):
        block = start // 8
        return jnp.concatenate([oc32[block], oc32[block + 4]], axis=0)

    hot1, hot2 = column_lines(first), column_lines(first + 256)
    hot = jnp.concatenate(
        [hot1[:, 0:256], hot2[:, 0:256], hot1[:, 256:384] + pltpu.roll(hot2[:, 256:384], 64, 1)],
        axis=1,
    )
    f_main, f_tail = states[8:16, 0:256], states[8:16, 256:384]
    fields_c = jnp.concatenate([f_main, f_main, f_tail + pltpu.roll(f_tail, 64, 1)], axis=1)[7:8]
    weight = jnp.where(second, line_weights(first + 256), line_weights(first))
    cols.gather1(residual(energy + fields_c, hot, residue_c, weight))
    rows.step4()
    cols.gather2()

    energy = rows.result()
    residue_rows = jnp.where(lane_r < 630, res_r, -1)
    block = core * 32 + y * 8 + z_hi
    hot = jnp.concatenate([or32[block], or32[block + 4]], axis=0)
    weight = line_weights(core * 256 + y * 64 + z_hi * 8)
    rows.gather1(residual(energy + fpad[0:1, :], hot, residue_rows, weight))
    cols.gather3()
    cols.gather4()
    rows.gather2()
    cols.gathered()

    def lines_of(source, first, lanes):
        return source[pl.ds(first, 32)].reshape(256, lanes).astype(BF16)

    whole = wc[...].reshape(256, 640)
    tail = whole[:, 512:640]
    tail_lane = lax.broadcasted_iota(jnp.int32, (1, 128), 1)
    tail1 = jnp.where(tail_lane < 64, tail, 0.0)
    tail2 = pltpu.roll(jnp.where(tail_lane < 64, 0.0, tail), 64, 1)
    first_c = jnp.concatenate([whole[:, 0:256], tail1], axis=1)
    second_c = jnp.concatenate([whole[:, 256:512], tail2], axis=1)
    total = None
    for n, lines in enumerate((first_c, second_c)):
        hot = lines_of(or32, 32 * n, 640)
        for piece in two_parts(lines):
            term = dot(hot, piece, ((0,), (0,)))
            total = term if total is None else total + term
    acc[...] = total

    rows.gather3()
    rows.gather4()

    last = []
    for h in range(2):
        own = wr.at[core, y, h]
        last.append(exchange(own, own, partner))
    for h in range(2):
        p, q = order(y, h)
        own = wr.at[core, q, h]
        last.append(exchange(own, own, partner))
    for h in range(2):
        p, q = order(y, h)
        for copy, i in zip(rows.g4[h], (p, far(y))):
            copy.wait_recv()
            own = wr.at[core, i, h]
            last.append(exchange(own, own, partner))

    def row_products(which):
        lines = wr[which].reshape(256, 640)
        hot = lines_of(oc32, which * 32, 384)
        high, low = two_parts(lines)
        sums = dot(high, hot, ((0,), (0,))) + dot(low, hot, ((0,), (0,)))
        return sums, jnp.sum(lines, axis=0, keepdims=True)

    sums, line_sum = row_products(core)
    acc[...] += sums
    for copy in last:
        copy.wait_recv()
    sums, other_sum = row_products(1 - core)
    fg_ref[...] = line_sum + other_sum
    total = acc[...] + sums
    g_ref[...] = total[0:630, 0:315]

    for copy in copies:
        copy.wait_send()

    @pl.when(row == owner)
    def _():
        for copy in state_copies:
            copy.wait_send()


def adam_update(values, first_moment, second_moment, gradient):
    first_new = 0.9 * first_moment + 0.1 * gradient
    second_new = 0.999 * second_moment + 0.001 * gradient * gradient
    change = (
        0.05 * (first_new / (1.0 - 0.9**10)) / (jnp.sqrt(second_new / (1.0 - 0.999**10)) + 1e-08)
    )
    return (values - change, first_new, second_new)


def on_device(
    alignment, seq_weight, couplings, pair_mean, pair_square, fields, field_mean, field_square
):
    vmem = pl.BlockSpec(memory_space=pltpu.VMEM)
    sums, field_sums = pl.pallas_call(
        kernel,
        out_shape=(
            jax.ShapeDtypeStruct(couplings.shape, F32),
            jax.ShapeDtypeStruct((1, 640), F32),
        ),
        in_specs=[vmem] * 4,
        out_specs=(vmem, vmem),
        scratch_shapes=[
            pltpu.VMEM((16, 512), F32),
            pltpu.VMEM((64, 8, 384), F32),
            pltpu.VMEM((64, 8, 640), F32),
            pltpu.VMEM((640, 384), BF16),
            pltpu.VMEM((640, 384), BF16),
        ]
        + [pltpu.VMEM((4, 2, 4, 8, 640), F32)] * 4
        + [
            pltpu.VMEM((2, 2, 4, 8, 640), F32),
            pltpu.VMEM((2, 4, 8, 640), F32),
            pltpu.VMEM((2, 2, 8, 640), F32),
            pltpu.VMEM((2, 8, 640), F32),
        ] * 2
        + [
            pltpu.VMEM((2, 4, 2, 4, 8, 640), F32),
            pltpu.VMEM((4, 2, 4, 8, 640), F32),
            pltpu.VMEM((640, 384), F32),
            pltpu.VMEM((8, 640), F32),
            pltpu.SemaphoreType.DMA((16,)),
            pltpu.SemaphoreType.DMA((72,)),
            pltpu.SemaphoreType.DMA((72,)),
        ],
        compiler_params=pltpu.CompilerParams(collective_id=0, has_side_effects=True),
    )(alignment, seq_weight.reshape(1, -1), couplings, fields.reshape(1, -1))
    row_residues = alignment.shape[1]
    column_residues = couplings.shape[1] // Q
    row_ids = (
        lax.axis_index("row") * row_residues
        + lax.broadcasted_iota(jnp.int32, (couplings.shape[0], 1), 0) // Q
    )
    column_ids = (
        lax.axis_index("col") * column_residues
        + lax.broadcasted_iota(jnp.int32, (1, couplings.shape[1]), 1) // Q
    )
    pair_grad = jnp.where(row_ids != column_ids, sums, 0.0) + 0.2 * (L - 1) * couplings
    field_grad = field_sums[0, : fields.shape[0]]
    new_pairs, new_pair_mean, new_pair_square = adam_update(
        couplings, pair_mean, pair_square, pair_grad
    )
    new_fields, new_field_mean, new_field_square = adam_update(
        fields, field_mean, field_square, field_grad
    )
    return (new_pairs, new_pair_mean, new_pair_square, new_fields, new_field_mean, new_field_square)


def solution(mesh):
    block = P("row", "col")
    in_specs = (P(None, "row"), P(), block, block, block, P("row"), P("row"), P("row"))
    out_specs = (block, block, block, P("row"), P("row"), P("row"))
    return jax.shard_map(
        on_device, mesh=mesh, in_specs=in_specs, out_specs=out_specs, check_vma=False
    )
```

time: 223 us -> 91.8 us (0.41)
  waiting for transfers between devices: 86.5 us -> 0 us
  Pallas kernels: 0 us -> 73.4 us
  blocking collectives: 59 us -> 0 us
  starting transfers between devices: 44 us -> 0 us
  matrix products: 9.56 us -> 0 us
  local copies, waits for them, and re-layouts: 17.9 us -> 12.1 us
    all_to_all x4 -> x0, waiting for transfers between devices: 86.5 us -> none  [the longest x2 39.5 us: copy_for_each(): return lax.all_to_all(copies, axis, split_axis=0, concat_axis=0, tiled=True)]
    pallas_call x0 -> x1, Pallas kernels: none -> 73.4 us  [on_device(): pl.pallas_call(kernel, out_shape=(jax.ShapeDtypeStruct(couplings.shape, F...]
    all_to_all x4 -> x0, starting transfers between devices: 44 us -> none  [the longest x2 25.5 us: copy_for_each(): return lax.all_to_all(copies, axis, split_axis=0, concat_axis=0, tiled=True)]
    all_gather x1 -> x0, blocking collectives: 39.9 us -> none  [from_root(): lax.all_gather(x, axis)]
    all_to_all x2 -> x0, blocking collectives: 19.2 us -> none  [the longest x1 12.5 us: sum_at_owner(): lax.all_to_all(blocks, axis, split_axis=0, concat_axis=0, tiled=True)]
    dot_general x8 -> x0, matrix products: 9.56 us -> none  [the longest x1 2.93 us: on_device(): lax.dot_general(row_onehot, column_weighted, contract, precision=lax.Prec...]
    unnamed x33 -> x23, local copies, waits for them, and re-layouts: 2.07 us -> 11.5 us
    eq x10 -> x0, local copies, waits for them, and re-layouts: 8.96 us -> none  [encode_states(): encoded = (states[:, :, None] == levels).astype(jnp.float32)]
  transfers between devices with their start and end apart: 4 -> 0, of which waited for: 4 -> 0; matrix products, arithmetic and copies ran while one was open for 3% -> 0% of each run, Pallas kernels for 0% -> 0%
where the time goes in v1:
time: 91.8 us; the launch traced here: 90.4 us
  Pallas kernels  73.4 us (80%)
  local copies, waits for them, and re-layouts  12.1 us (13%)
  other arithmetic  4.23 us (5%)
    pallas_call x1, Pallas kernels, on_device(): pl.pallas_call(kernel, out_shape=(jax.ShapeDtypeStruct(couplings.shape, F...  73.4 us
    unnamed x23, local copies, waits for them, and re-layouts  11.5 us
    sub x2, other arithmetic, adam_update(): return (values - change, first_new, second_new)  4.2 us

profile of v1, /device:TPU:1, one launch (start us, length us, event | category | flops | bytes accessed | tf_op | source)
XLA Modules:
  0.0 90.4 jit_solution(6753749099910764377)
XLA Ops:
  0.6 0.0 copy-start.3
  0.6 0.0 copy-start.4
  0.7 2.5 %copy.19.j_ref = f32[630,315]{1,0:T(8,128)} copy(f32[630,315]{0,1:T(8,128)} %param.10) | data formatting | bytes 1587600 | tf_op args[2]
  3.2 0.0 copy-done.3
  3.2 0.0 copy-start.1
  3.2 0.8 copy.15.al_ref
  4.0 0.0 copy-done.4
  4.0 0.6 reshape.69.f_ref
  4.6 73.4 %shard_map.127 = (f32[630,315]{1,0:T(8,128)}, f32[1,640]{1,0:T(1,128)}) custom-call(s32[512,30]{1,0:T(8,128)} %copy.15.al_ref, f32[1,512]{1,0:T(1,128)} %bitcast.1, f32[630,315]{1,0:T(8,128)} %copy.19.j_ref, f32[1,630]{1,0:T(1,128)} %reshape.69.f_ref), custom_call_target="tpu_custom_call" | custom-call | tf_op jit(solution)/shard_map/pallas_call | solution.py:413
  78.1 0.0 copy-done.1
  78.1 0.0 copy-start.2
  78.1 1.3 %copy.14 = f32[630,315]{1,0:T(8,128)} copy(f32[630,315]{0,1:T(8,128)S(1)} %copy-done.1) | data formatting | bytes 1587600 | tf_op args[3]
  79.4 0.0 copy-done.2
  79.4 0.0 copy-start
  79.4 1.3 %copy.18 = f32[630,315]{1,0:T(8,128)} copy(f32[630,315]{0,1:T(8,128)S(1)} %copy-done.2) | data formatting | bytes 1587600 | tf_op args[4]
  80.7 0.0 copy-done
  80.7 3.6 %divide_subtract_fusion = (f32[630,315]{1,0:T(8,128)}, f32[630,315]{1,0:T(8,128)S(1)}, f32[630,315]{1,0:T(8,128)S(1)}) fusion(f32[630,315]{1,0:T(8,128)S(1)} %copy-done, f32[630,315]{1,0:T(8,128)} %get-tuple-element.8, s32[315]{0:T(512)S(1)} %fusion.6, s32[630]{0:T(1024)S(1)} %fusion.1, f32[630,315]{1,0:T(8,128)} %copy.14, f32[630,315]{1,0:T(8,128)} %copy.18), kind=kLoop, calls=%fused_computation.2 | loop fusion | flops 3175200 | bytes 5560380 | tf_op jit(solution)/shard_map/sub | solution.py:406
  84.3 2.4 %copy.20 = f32[630,315]{0,1:T(8,128)} copy(f32[630,315]{1,0:T(8,128)} %get-tuple-element.19) | data formatting | bytes 1587600
  86.7 1.2 %copy.21 = f32[630,315]{0,1:T(8,128)} copy(f32[630,315]{1,0:T(8,128)S(1)} %get-tuple-element.20) | data formatting | bytes 1587600
  87.9 0.0 copy-start.7
  87.9 1.2 %copy.22 = f32[630,315]{0,1:T(8,128)} copy(f32[630,315]{1,0:T(8,128)S(1)} %get-tuple-element.21) | data formatting | bytes 1587600
  89.1 0.0 copy-start.5
  89.1 0.0 copy-start.6
  89.1 0.0 copy-done.7
  89.1 0.7 copy-done.5
  89.8 0.0 copy-done.6
  89.8 0.6 divide_subtract_fusion.1
  (3 shorter events, 0.0 us)
Async XLA Ops:
  0.6 2.5 %copy-start.3 = (s32[512,30]{0,1:T(8,128)S(1)}, s32[512,30]{0,1:T(8,128)}, u32[]{:S(2)}) copy-start(s32[512,30]{0,1:T(8,128)} %param.8) | copy-start | bytes 184324
  0.6 3.4 %copy-start.4 = (f32[630]{0:T(1024)S(1)}, f32[630]{0:T(1024)}, u32[]{:S(2)}) copy-start(f32[630]{0:T(1024)} %param.13) | copy-start | bytes 7564
  3.2 74.9 %copy-start.1 = (f32[630,315]{0,1:T(8,128)S(1)}, f32[630,315]{0,1:T(8,128)}, u32[]{:S(2)}) copy-start(f32[630,315]{0,1:T(8,128)} %param.11) | copy-start | bytes 2381404
  78.1 1.3 %copy-start.2 = (f32[630,315]{0,1:T(8,128)S(1)}, f32[630,315]{0,1:T(8,128)}, u32[]{:S(2)}) copy-start(f32[630,315]{0,1:T(8,128)} %param.12) | copy-start | bytes 2381404
  79.4 1.3 %copy-start = (f32[630,315]{1,0:T(8,128)S(1)}, f32[630,315]{1,0:T(8,128)}, u32[]{:S(2)}) copy-start(f32[630,315]{1,0:T(8,128)} %copy.19.j_ref) | copy-start | bytes 2381404
  87.9 1.2 %copy-start.7 = (f32[1,640]{1,0:T(1,128)S(1)}, f32[1,640]{1,0:T(1,128)}, u32[]{:S(2)}) copy-start(f32[1,640]{1,0:T(1,128)} %get-tuple-element.9) | copy-start | bytes 7684
  89.1 0.7 copy-start.5
  89.1 0.7 copy-start.6

commit v2 on v1

v2 whole, which is shorter than its diff:
```python
import jax
import jax.numpy as jnp
from jax import lax
from jax.experimental import pallas as pl
from jax.experimental.pallas import tpu as pltpu
from jax.sharding import PartitionSpec as P

L = 480
Q = 21
MESH = pl.DeviceIdType.MESH
F32 = jnp.float32
BF16 = jnp.bfloat16
ROW_GROUPS = ((0, 384), (384, 640))


def two_parts(x):
    high = x.astype(BF16)
    return high, (x - high.astype(F32)).astype(BF16)


def three_parts(x):
    high = x.astype(BF16)
    rest = x - high.astype(F32)
    mid = rest.astype(BF16)
    return high, mid, (rest - mid.astype(F32)).astype(BF16)


def dot(a, b, dims=((1,), (0,))):
    return lax.dot_general(a, b, (dims, ((), ())), preferred_element_type=F32)


def residue_of(lane):
    return ((lane.astype(F32) + 0.5) * (1.0 / Q)).astype(jnp.int32)


def flip(i):
    return i + 1 - 2 * (i % 2)


def mirror(i):
    return 3 - i


def packed_column(lane):
    main = jnp.where(lane < 256, lane, lane - 256)
    tail = jnp.where(lane < 576, lane - 512, lane - 576)
    column = jnp.where(lane < 512, main, tail + 256)
    second = ((lane >= 256) & (lane < 512)) | (lane >= 576)
    return column, second, (lane < 512) | (tail < 59)


def iota(shape, dim):
    return lax.broadcasted_iota(jnp.int32, shape, dim)


def as_bf16(mask):
    return mask.astype(F32).astype(BF16)


def order(i, half):
    first, second = flip(i), mirror(i)
    return (first, second) if half == 0 else (second, first)


def far(i):
    return (i + 2) % 4


class Reduce:
    def __init__(self, exchange, a, b, at, total, ins, full, groups):
        self.exchange, self.a, self.b, self.at = exchange, a, b, at
        self.total, self.ins, self.full, self.groups = total, ins, full, groups
        self.s1, self.s2, self.s3, self.s4 = {}, {}, {}, {}
        self.g1, self.g2, self.g3 = {}, {}, {}

    def lanes(self, g):
        low, high = self.groups[g]
        return pl.ds(low, high - low)

    def step1(self, g):
        at = self.lanes(g)
        for h in range(2):
            p, _ = order(self.a, h)
            to = self.at(p, self.b)
            later = self.total.at[far(self.a), h, :, :, at]
            theirs = self.total.at[p, h, :, :, at]
            one = self.exchange(later, self.ins[0].at[h, 1, :, :, at], to)
            two = self.exchange(theirs, self.ins[0].at[h, 0, :, :, at], to)
            self.s1[g, h] = (two, one)

    def step2(self, g):
        at = self.lanes(g)
        for h in range(2):
            p, q = order(self.a, h)
            self.s1[g, h][1].wait_recv()
            self.total[q, h, :, :, at] += self.ins[0][h, 1, :, :, at]
            self.s2[g, h] = self.exchange(
                self.total.at[q, h, :, :, at], self.ins[1].at[h, :, :, at], self.at(q, self.b)
            )
        for h in range(2):
            self.s1[g, h][0].wait_recv()
            self.total[self.a, h, :, :, at] += self.ins[0][h, 0, :, :, at]

    def step3(self, g):
        at = self.lanes(g)
        for h in range(2):
            p, _ = order(self.b, h)
            self.s2[g, h].wait_recv()
            self.total[self.a, h, :, :, at] += self.ins[1][h, :, :, at]
            to = self.at(self.a, p)
            self.s3[g, h] = [
                self.exchange(self.total.at[self.a, h, i, :, at], self.ins[2].at[h, n, :, at], to)
                for n, i in enumerate((p, far(self.b)))
            ]

    def step4(self, g):
        at = self.lanes(g)
        for h in range(2):
            p, q = order(self.b, h)
            to = self.at(self.a, q)
            for n, i in enumerate((self.b, q)):
                self.s3[g, h][n].wait_recv()
                self.total[self.a, h, i, :, at] += self.ins[2][h, n, :, at]
            self.s4[g, h] = [
                self.exchange(self.total.at[self.a, h, i, :, at], self.ins[3].at[h, 1 - n, :, at], to)
                for n, i in enumerate((self.b, q))
            ]

    def blocks(self):
        return [(h, i) for h in range(2) for i in (self.b, order(self.b, h)[1])]

    def result(self):
        for sent in self.s4.values():
            for copy in sent:
                copy.wait_recv()
        parts = [
            self.total[self.a, h, i] + self.ins[3][h, n % 2] for n, (h, i) in enumerate(self.blocks())
        ]
        return jnp.concatenate(parts, axis=0)

    def gather1(self, value):
        for n, (h, i) in enumerate(self.blocks()):
            self.full[self.a, h, i] = value[8 * n : 8 * n + 8]
        for g in range(len(self.groups)):
            at = self.lanes(g)
            for h in range(2):
                p, q = order(self.b, h)
                self.g1[g, h] = [
                    self.exchange(
                        self.full.at[self.a, h, i, :, at],
                        self.full.at[self.a, h, i, :, at],
                        self.at(self.a, p),
                    )
                    for i in (self.b, q)
                ]

    def gather2(self, g):
        at = self.lanes(g)
        for h in range(2):
            p, q = order(self.a, h)
            for copy in self.g1[g, h]:
                copy.wait_recv()
            own = self.full.at[self.a, h, :, :, at]
            self.g2[g, h] = self.exchange(own, own, self.at(q, self.b))
            self.g3[g, h] = [self.exchange(own, own, self.at(p, self.b))]

    def gather3(self, g):
        at = self.lanes(g)
        for h in range(2):
            p, q = order(self.a, h)
            second = self.full.at[q, h, :, :, at]
            self.g2[g, h].wait_recv()
            self.g3[g, h].append(self.exchange(second, second, self.at(p, self.b)))

    def gathered(self, g):
        for h in range(2):
            for copy in self.g3[g, h]:
                copy.wait_recv()


def kernel(
    al_ref, w_ref, j_ref, f_ref, g_ref, fg_ref,
    states, oc32, or32, oct, j_high, j_low, j_in, xr, xc,
    r_in1, r_in2, r_in3, r_in4, c_in1, c_in2, c_in3, c_in4, wr, wc, acc,
    fpad, state_send, send, recv,
):
    row, col = lax.axis_index("row"), lax.axis_index("col")
    z_lo, x = row // 4, row % 4
    y, z_hi, core = col // 8, (col // 2) % 4, col % 2
    owner = col // 2

    def at_row(a, b):
        return (row, a * 8 + b * 2 + core)

    def at_col(a, b):
        return (b * 4 + a, col)

    partner = (row, y * 8 + z_hi * 2 + 1 - core)

    barrier = pltpu.get_barrier_semaphore()
    greeted = [at_row(flip(y), z_hi), at_row(mirror(y), z_hi), at_row(y, flip(z_hi))]
    greeted += [at_row(y, mirror(z_hi)), partner]
    greeted += [((row + d) % 16, col) for d in range(1, 16)]
    for device in greeted:
        pl.semaphore_signal(barrier, inc=1, device_id=device, device_id_type=MESH)

    fpad[...] = jnp.zeros_like(fpad)
    fpad[0:1, 0:630] = f_ref[...]
    fields = fpad[...]
    field_lane = iota((8, 640), 1)
    fields0 = jnp.where(field_lane < 315, fields, 0.0)[0:1, 0:512]
    fields1 = jnp.where(field_lane < 315, pltpu.roll(fields, 325, 1), 0.0)[0:1, 0:512]
    alignment = al_ref[...].astype(F32).astype(BF16)
    word_row, word_residue = iota((8, 30), 0), iota((8, 30), 1)
    digit = word_residue - 5 * word_row
    scale = jnp.zeros((8, 30), F32)
    for d in range(5):
        scale = jnp.where(digit == d, float(Q**d), scale)
    words = sum(dot(part, alignment) for part in three_parts(scale))
    word_line = iota((8, 512), 0)
    words = jnp.where(word_line == 6, fields0, jnp.where(word_line == 7, fields1, words))

    pl.semaphore_wait(barrier, len(greeted))

    state_copies = [
        pltpu.make_async_remote_copy(
            states, states, state_send.at[d], recv.at[0],
            device_id=((row + d) % 16, col), device_id_type=MESH,
        )
        for d in range(1, 16)
    ]

    @pl.when(row == owner)
    def _():
        states[...] = words
        for copy in state_copies:
            copy.start()

    copies = []

    def exchange(src, dst, device):
        at = len(copies) + 1
        copy = pltpu.make_async_remote_copy(
            src, dst, send.at[at], recv.at[at], device_id=device, device_id_type=MESH
        )
        copy.start()
        copies.append(copy)
        return copy

    across = exchange(j_ref, j_in, partner)
    j_high[...] = jnp.zeros_like(j_high)
    j_low[...] = jnp.zeros_like(j_low)
    high, low = two_parts(j_ref[...])
    j_high[0:315, 0:630] = high
    j_low[0:315, 0:630] = low

    lane_r = iota((1, 640), 1)
    res_r = residue_of(lane_r)
    spread_r = iota((30, 640), 0) == residue_of(iota((30, 640), 1))
    value_r = dot(alignment, as_bf16(spread_r), ((0,), (0,)))
    hot_r = (value_r == (lane_r - res_r * Q).astype(F32)) & (lane_r < 630)
    hot_r = hot_r.astype(F32)
    or32[...] = hot_r.reshape(64, 8, 640)
    hot_r = hot_r.astype(BF16)

    nt = ((1,), (1,))
    top, bottom = hot_r[0:256], hot_r[256:512]
    none = jnp.zeros((64, 640), BF16)
    tails = [j[256:320] for j in (j_high, j_low)]
    tails1 = [jnp.concatenate([tail, none], axis=0) for tail in tails]
    tails2 = [jnp.concatenate([none, tail], axis=0) for tail in tails]
    mains = [j[0:256] for j in (j_high, j_low)]
    xc[:, :, :, :, 0:256] = sum(dot(top, j, nt) for j in mains).reshape(4, 2, 4, 8, 256)
    xc[:, :, :, :, 256:512] = sum(dot(bottom, j, nt) for j in mains).reshape(4, 2, 4, 8, 256)
    xc[:, :, :, :, 512:640] = (
        sum(dot(top, j, nt) for j in tails1) + sum(dot(bottom, j, nt) for j in tails2)
    ).reshape(4, 2, 4, 8, 128)

    cols = Reduce(
        exchange, x, z_lo, at_col, xc, (c_in1, c_in2, c_in3, c_in4), wc, ((0, 640),)
    )
    rows = Reduce(
        exchange, y, z_hi, at_row, xr, (r_in1, r_in2, r_in3, r_in4), wr.at[core], ROW_GROUPS
    )
    row_groups = range(len(ROW_GROUPS))
    cols.step1(0)

    across.wait_recv()
    high, low = two_parts(j_in[...])
    j_high[320:635, 0:630] = high
    j_low[320:635, 0:630] = low

    @pl.when(row != owner)
    def _():
        state_copies[0].wait_recv()

    rest = jnp.where(word_line < 6, states[...], 0.0)
    digits = []
    for _ in range(4):
        quotient = jnp.floor(rest * (1.0 / Q))
        remainder = rest - quotient * Q
        over, under = remainder >= Q, remainder < 0.0
        quotient = jnp.where(over, quotient + 1.0, jnp.where(under, quotient - 1.0, quotient))
        remainder = jnp.where(over, remainder - Q, jnp.where(under, remainder + Q, remainder))
        digits.append(remainder)
        rest = quotient
    digits = jnp.concatenate(digits + [rest], axis=0).astype(BF16)

    def digit_residue(shape, dim):
        at = iota(shape, dim)
        line = at % 8
        return jnp.where(line < 6, 5 * line + at // 8, -1)

    lane_b = iota((40, 640), 1)
    block_b = jnp.where(lane_b < 320, core, 1 - core)
    local_b = jnp.where(lane_b < 320, lane_b, lane_b - 320)
    spread_b = digit_residue((40, 640), 0) == block_b * 15 + residue_of(local_b)
    own_digits = jnp.where(core == 0, digits[:, 0:256].astype(F32), digits[:, 256:512].astype(F32))
    value_b = dot(own_digits.astype(BF16), as_bf16(spread_b), ((0,), (0,)))
    local = jnp.where(lane_r < 320, lane_r, lane_r - 320)
    hot_b = (value_b == (local - residue_of(local) * Q).astype(F32)) & (local < 315)
    hot_b = as_bf16(hot_b)
    for g in row_groups:
        at = rows.lanes(g)
        sums = dot(hot_b, j_high[:, at]) + dot(hot_b, j_low[:, at])
        xr[:, :, :, :, at] = sums.reshape(4, 2, 4, 8, -1)
        rows.step1(g)

    lane_c = iota((1, 384), 1)
    spread_c = digit_residue((40, 384), 0) == core * 15 + residue_of(iota((40, 384), 1))
    value_c = dot(digits, as_bf16(spread_c), ((0,), (0,)))
    hot_c = (value_c == (lane_c - residue_of(lane_c) * Q).astype(F32)) & (lane_c < 315)
    oc32[...] = hot_c.astype(F32).reshape(64, 8, 384)
    line_c = iota((320, 1), 0)
    spread_t = digit_residue((320, 40), 1) == core * 15 + residue_of(iota((320, 40), 0))
    value_t = dot(as_bf16(spread_t), digits)
    hot_t = (value_t == (line_c - residue_of(line_c) * Q).astype(F32)) & (line_c < 315)
    hot_t = as_bf16(hot_t)
    oct[0] = hot_t[:, 0:256]
    oct[1] = hot_t[:, 256:512]

    cols.step2(0)
    for g in row_groups:
        rows.step2(g)
    cols.step3(0)
    for g in row_groups:
        rows.step3(g)
    cols.step4(0)

    def line_weights(first):
        lane = iota((8, 512), 1) - iota((8, 512), 0)
        found = [jnp.where(lane == first + 32 * h + 8 * i, w_ref[...], 0.0) for h, i in first_blocks]
        return jnp.sum(jnp.concatenate(found, axis=0), axis=1, keepdims=True)

    def residual(energy, hot, residue, weight):
        member = as_bf16(iota((128, 640), 0) == residue)
        powers = jnp.exp(energy)
        lines = energy.shape[0]
        parts = dot(jnp.concatenate(three_parts(powers), axis=0), member, nt)
        sums = parts[0:lines] + parts[lines : 2 * lines] + parts[2 * lines :]
        inverse = jnp.where(sums > 0.0, 1.0 / sums, 0.0)
        parts = dot(jnp.concatenate(three_parts(inverse), axis=0), member)
        inverse = parts[0:lines] + parts[lines : 2 * lines] + parts[2 * lines :]
        return weight * (powers * inverse - hot)

    column, second, valid = packed_column(lane_r)
    residue_c = jnp.where(valid, residue_of(column) + jnp.where(second, 32, 0), -1)
    first = x * 64
    first_blocks = cols.blocks()

    def column_lines(start):
        return jnp.concatenate([oc32[start // 8 + 4 * h + i] for h, i in cols.blocks()], axis=0)

    hot1, hot2 = column_lines(first), column_lines(first + 256)
    hot = jnp.concatenate(
        [hot1[:, 0:256], hot2[:, 0:256], hot1[:, 256:384] + pltpu.roll(hot2[:, 256:384], 64, 1)],
        axis=1,
    )
    fields_c = jnp.where(core == 0, states[6:7, :], states[7:8, :])
    f_main, f_tail = fields_c[:, 0:256], jnp.broadcast_to(fields_c[:, 256:384], (8, 128))
    f_tail = (f_tail + pltpu.roll(f_tail, 64, 1))[0:1]
    fields_c = jnp.concatenate([f_main, f_main, f_tail], axis=1)
    weight = jnp.where(second, line_weights(first + 256), line_weights(first))
    cols.gather1(residual(cols.result() + fields_c, hot, residue_c, weight))
    for g in row_groups:
        rows.step4(g)
    cols.gather2(0)
    cols.gather3(0)

    residue_rows = jnp.where(lane_r < 630, res_r, -1)
    block = core * 32 + y * 8
    hot = jnp.concatenate([or32[block + 4 * h + i] for h, i in rows.blocks()], axis=0)
    first_blocks = rows.blocks()
    weight = line_weights(core * 256 + y * 64)
    rows.gather1(residual(rows.result() + fpad[0:1, :], hot, residue_rows, weight))

    cols.gathered(0)
    whole = wc[...].reshape(256, 640)
    tail = whole[:, 512:640]
    tail_lane = iota((1, 128), 1)
    tail1 = jnp.where(tail_lane < 64, tail, 0.0)
    tail2 = pltpu.roll(jnp.where(tail_lane < 64, 0.0, tail), 64, 1)
    first_c = jnp.concatenate([whole[:, 0:256], tail1], axis=1)
    second_c = jnp.concatenate([whole[:, 256:512], tail2], axis=1)

    def products(n, lines):
        hot = or32[32 * n : 32 * n + 32].reshape(256, 640).astype(BF16)
        return sum(dot(piece, hot, ((0,), (0,))) for piece in two_parts(lines))

    acc[...] = products(0, first_c) + products(1, second_c)

    for g in row_groups:
        rows.gather2(g)
    last = []

    def forward(i, h, g):
        piece = wr.at[core, i, h, :, :, rows.lanes(g)]
        last.append(exchange(piece, piece, partner))

    for g in row_groups:
        rows.gather3(g)
        for h in range(2):
            forward(y, h, g)
            forward(order(y, h)[1], h, g)
    for g in row_groups:
        rows.gathered(g)
        for h in range(2):
            forward(order(y, h)[0], h, g)
            forward(far(y), h, g)

    def row_products(which):
        lines = wr[which].reshape(256, 640)
        hot = oct[which]
        sums = sum(dot(hot, piece) for piece in two_parts(lines))
        return sums, jnp.sum(lines, axis=0, keepdims=True)

    sums, line_sum = row_products(core)
    acc[0:320, :] += sums
    for copy in last:
        copy.wait_recv()
    sums, other_sum = row_products(1 - core)
    fg_ref[...] = line_sum + other_sum
    total = acc[0:320, :] + sums
    g_ref[...] = total[0:315, 0:630]

    for copy in copies:
        copy.wait_send()

    @pl.when(row == owner)
    def _():
        for copy in state_copies:
            copy.wait_send()


def adam_update(values, first_moment, second_moment, gradient):
    first_new = 0.9 * first_moment + 0.1 * gradient
    second_new = 0.999 * second_moment + 0.001 * gradient * gradient
    change = (
        0.05 * (first_new / (1.0 - 0.9**10)) / (jnp.sqrt(second_new / (1.0 - 0.999**10)) + 1e-08)
    )
    return (values - change, first_new, second_new)


def on_device(
    alignment, seq_weight, couplings, pair_mean, pair_square, fields, field_mean, field_square
):
    vmem = pl.BlockSpec(memory_space=pltpu.VMEM)
    sums, field_sums = pl.pallas_call(
        kernel,
        out_shape=(
            jax.ShapeDtypeStruct(couplings.shape[::-1], F32),
            jax.ShapeDtypeStruct((1, 640), F32),
        ),
        in_specs=[vmem] * 4,
        out_specs=(vmem, vmem),
        scratch_shapes=[
            pltpu.VMEM((8, 512), F32),
            pltpu.VMEM((64, 8, 384), F32),
            pltpu.VMEM((64, 8, 640), F32),
            pltpu.VMEM((2, 320, 256), BF16),
            pltpu.VMEM((640, 640), BF16),
            pltpu.VMEM((640, 640), BF16),
            pltpu.VMEM(couplings.shape[::-1], F32),
        ]
        + [pltpu.VMEM((4, 2, 4, 8, 640), F32)] * 2
        + [
            pltpu.VMEM((2, 2, 4, 8, 640), F32),
            pltpu.VMEM((2, 4, 8, 640), F32),
            pltpu.VMEM((2, 2, 8, 640), F32),
            pltpu.VMEM((2, 2, 8, 640), F32),
        ] * 2
        + [
            pltpu.VMEM((2, 4, 2, 4, 8, 640), F32),
            pltpu.VMEM((4, 2, 4, 8, 640), F32),
            pltpu.VMEM((384, 640), F32),
            pltpu.VMEM((8, 640), F32),
            pltpu.SemaphoreType.DMA((16,)),
            pltpu.SemaphoreType.DMA((96,)),
            pltpu.SemaphoreType.DMA((96,)),
        ],
        compiler_params=pltpu.CompilerParams(collective_id=0, has_side_effects=True),
    )(alignment.T, seq_weight.reshape(1, -1), couplings.T, fields.reshape(1, -1))
    sums = sums.T
    row_residues = alignment.shape[1]
    column_residues = couplings.shape[1] // Q
    row_ids = (
        lax.axis_index("row") * row_residues
        + lax.broadcasted_iota(jnp.int32, (couplings.shape[0], 1), 0) // Q
    )
    column_ids = (
        lax.axis_index("col") * column_residues
        + lax.broadcasted_iota(jnp.int32, (1, couplings.shape[1]), 1) // Q
    )
    pair_grad = jnp.where(row_ids != column_ids, sums, 0.0) + 0.2 * (L - 1) * couplings
    field_grad = field_sums[0, : fields.shape[0]]
    new_pairs, new_pair_mean, new_pair_square = adam_update(
        couplings, pair_mean, pair_square, pair_grad
    )
    new_fields, new_field_mean, new_field_square = adam_update(
        fields, field_mean, field_square, field_grad
    )
    return (new_pairs, new_pair_mean, new_pair_square, new_fields, new_field_mean, new_field_square)


def solution(mesh):
    block = P("row", "col")
    in_specs = (P(None, "row"), P(), block, block, block, P("row"), P("row"), P("row"))
    out_specs = (block, block, block, P("row"), P("row"), P("row"))
    return jax.shard_map(
        on_device, mesh=mesh, in_specs=in_specs, out_specs=out_specs, check_vma=False
    )
```

time: 91.8 us -> 72.2 us (0.79); the launches traced: 90.4 us -> 71.9 us
  local copies, waits for them, and re-layouts: 12.1 us -> 2.04 us
  Pallas kernels: 73.4 us -> 64.9 us
    unnamed x23 -> x10, local copies, waits for them, and re-layouts: 11.5 us -> 0.69 us
    pallas_call x1, Pallas kernels: 73.4 us -> 64.9 us  [on_device(): pl.pallas_call(kernel, out_shape=(jax.ShapeDtypeStruct(couplings.shape[::...]
where the time goes in v2:
time: 72.2 us; the launch traced here: 71.9 us
  Pallas kernels  64.9 us (90%)
  other arithmetic  4.24 us (6%)
  local copies, waits for them, and re-layouts  2.04 us (3%)
    pallas_call x1, Pallas kernels, on_device(): pl.pallas_call(kernel, out_shape=(jax.ShapeDtypeStruct(couplings.shape[::...  64.9 us
    sub x2, other arithmetic, adam_update(): return (values - change, first_new, second_new)  4.22 us

profile of v2, /device:TPU:1, one launch (start us, length us, event | category | flops | bytes accessed | tf_op | source)
XLA Modules:
  0.0 71.9 jit_solution(17310241525216258310)
XLA Ops:
  0.6 0.0 copy-start
  0.6 1.3 %reshape.69.f_ref = f32[1,630]{1,0:T(1,128)} reshape(f32[630]{0:T(1024)} %param.13) | data formatting | bytes 5040 | tf_op jit(solution)/shard_map/reshape | solution.py:502
  2.0 64.9 %shard_map.127 = (f32[315,630]{1,0:T(8,128)}, f32[1,640]{1,0:T(1,128)}) custom-call(s32[30,512]{1,0:T(8,128)} %bitcast.14, f32[1,512]{1,0:T(1,128)} %bitcast.15, f32[315,630]{1,0:T(8,128)} %bitcast.13, f32[1,630]{1,0:T(1,128)} %reshape.69.f_ref), custom_call_target="tpu_custom_call" | custom-call | tf_op jit(solution)/shard_map/pallas_call | solution.py:468
  67.0 0.0 copy-done
  67.0 0.0 copy-start.3
  67.0 3.6 %divide_subtract_fusion = (f32[630,315]{0,1:T(8,128)}, f32[630,315]{0,1:T(8,128)}, f32[630,315]{0,1:T(8,128)}) fusion(f32[630,315]{0,1:T(8,128)S(1)} %copy-done, f32[315,630]{1,0:T(8,128)} %get-tuple-element.8, s32[315]{0:T(512)S(1)} %fusion.7, s32[630]{0:T(1024)S(1)} %fusion.2, f32[630,315]{0,1:T(8,128)} %param.11, f32[630,315]{0,1:T(8,128)} %param.12), kind=kLoop, calls=%fused_computation.4 | loop fusion | flops 3175200 | bytes 5560380 | tf_op jit(solution)/shard_map/sub | solution.py:461
  70.6 0.0 copy-start.4
  70.6 0.0 copy-start.1
  70.6 0.0 copy-start.2
  70.6 0.7 copy-done.4
  71.3 0.0 copy-done.3
  71.3 0.0 copy-done.1
  71.3 0.0 copy-done.2
  71.3 0.6 divide_subtract_fusion.1
  (3 shorter events, 0.0 us)
Async XLA Ops:
  0.6 66.4 %copy-start = (f32[630,315]{0,1:T(8,128)S(1)}, f32[630,315]{0,1:T(8,128)}, u32[]{:S(2)}) copy-start(f32[630,315]{0,1:T(8,128)} %param.10) | copy-start | bytes 2381404
  67.0 4.3 %copy-start.3 = (f32[630]{0:T(1024)S(1)}, f32[630]{0:T(1024)}, u32[]{:S(2)}) copy-start(f32[630]{0:T(1024)} %param.15) | copy-start | bytes 7564
  70.6 0.7 copy-start.4
  70.6 0.7 copy-start.1
  70.6 0.7 copy-start.2

commit v3 on v2

--- a/solution.py
+++ b/solution.py
@@ -10,6 +10,7 @@
 MESH = pl.DeviceIdType.MESH
 F32 = jnp.float32
 BF16 = jnp.bfloat16
+VMEM_LIMIT = 24 * 2**20
 ROW_GROUPS = ((0, 384), (384, 640))
 
 
@@ -179,10 +180,10 @@
 
 
 def kernel(
-    al_ref, w_ref, j_ref, f_ref, g_ref, fg_ref,
+    al_in, w_in, j_ref, f_in, g_ref, fg_ref,
     states, oc32, or32, oct, j_high, j_low, j_in, xr, xc,
     r_in1, r_in2, r_in3, r_in4, c_in1, c_in2, c_in3, c_in4, wr, wc, acc,
-    fpad, state_send, send, recv,
+    fpad, al_ref, w_ref, j_own, f_ref, local, state_send, send, recv,
 ):
     row, col = lax.axis_index("row"), lax.axis_index("col")
     z_lo, x = row // 4, row % 4
@@ -204,8 +205,19 @@
     for device in greeted:
         pl.semaphore_signal(barrier, inc=1, device_id=device, device_id_type=MESH)
 
+    loads = [
+        pltpu.make_async_copy(src, dst, local.at[n])
+        for n, (src, dst) in enumerate(
+            ((al_in, al_ref), (f_in, f_ref), (j_ref, j_own), (w_in, w_ref))
+        )
+    ]
+    for load in loads:
+        load.start()
+    loads[0].wait()
+    loads[1].wait()
+
     fpad[...] = jnp.zeros_like(fpad)
-    fpad[0:1, 0:630] = f_ref[...]
+    fpad[0:1, 0:630] = f_ref[...].reshape(1, 630)
     fields = fpad[...]
     field_lane = iota((8, 640), 1)
     fields0 = jnp.where(field_lane < 315, fields, 0.0)[0:1, 0:512]
@@ -250,7 +262,9 @@
     across = exchange(j_ref, j_in, partner)
     j_high[...] = jnp.zeros_like(j_high)
     j_low[...] = jnp.zeros_like(j_low)
-    high, low = two_parts(j_ref[...])
+    loads[2].wait()
+    loads[3].wait()
+    high, low = two_parts(j_own[...])
     j_high[0:315, 0:630] = high
     j_low[0:315, 0:630] = low
 
@@ -347,6 +361,9 @@
         rows.step3(g)
     cols.step4(0)
 
+    for g in row_groups:
+        rows.step4(g)
+
     def line_weights(first):
         lane = iota((8, 512), 1) - iota((8, 512), 0)
         found = [jnp.where(lane == first + 32 * h + 8 * i, w_ref[...], 0.0) for h, i in first_blocks]
@@ -382,10 +399,7 @@
     fields_c = jnp.concatenate([f_main, f_main, f_tail], axis=1)
     weight = jnp.where(second, line_weights(first + 256), line_weights(first))
     cols.gather1(residual(cols.result() + fields_c, hot, residue_c, weight))
-    for g in row_groups:
-        rows.step4(g)
     cols.gather2(0)
-    cols.gather3(0)
 
     residue_rows = jnp.where(lane_r < 630, res_r, -1)
     block = core * 32 + y * 8
@@ -393,6 +407,10 @@
     first_blocks = rows.blocks()
     weight = line_weights(core * 256 + y * 64)
     rows.gather1(residual(rows.result() + fpad[0:1, :], hot, residue_rows, weight))
+
+    cols.gather3(0)
+    for g in row_groups:
+        rows.gather2(g)
 
     cols.gathered(0)
     whole = wc[...].reshape(256, 640)
@@ -407,10 +425,7 @@
         hot = or32[32 * n : 32 * n + 32].reshape(256, 640).astype(BF16)
         return sum(dot(piece, hot, ((0,), (0,))) for piece in two_parts(lines))
 
-    acc[...] = products(0, first_c) + products(1, second_c)
-
-    for g in row_groups:
-        rows.gather2(g)
+    acc[...] = products(0, first_c)
     last = []
 
     def forward(i, h, g):
@@ -422,6 +437,7 @@
         for h in range(2):
             forward(y, h, g)
             forward(order(y, h)[1], h, g)
+    acc[...] += products(1, second_c)
     for g in row_groups:
         rows.gathered(g)
         for h in range(2):
@@ -471,7 +487,7 @@
             jax.ShapeDtypeStruct(couplings.shape[::-1], F32),
             jax.ShapeDtypeStruct((1, 640), F32),
         ),
-        in_specs=[vmem] * 4,
+        in_specs=[pl.BlockSpec(memory_space=pltpu.HBM)] * 4,
         out_specs=(vmem, vmem),
         scratch_shapes=[
             pltpu.VMEM((8, 512), F32),
@@ -494,12 +510,20 @@
             pltpu.VMEM((4, 2, 4, 8, 640), F32),
             pltpu.VMEM((384, 640), F32),
             pltpu.VMEM((8, 640), F32),
+            pltpu.VMEM(alignment.shape[::-1], jnp.int32),
+            pltpu.VMEM((1, 512), F32),
+            pltpu.VMEM(couplings.shape[::-1], F32),
+            pltpu.VMEM(fields.shape, F32),
+            pltpu.SemaphoreType.DMA((4,)),
             pltpu.SemaphoreType.DMA((16,)),
             pltpu.SemaphoreType.DMA((96,)),
             pltpu.SemaphoreType.DMA((96,)),
         ],
-        compiler_params=pltpu.CompilerParams(collective_id=0, has_side_effects=True),
-    )(alignment.T, seq_weight.reshape(1, -1), couplings.T, fields.reshape(1, -1))
+        compiler_params=pltpu.CompilerParams(collective_id=0, has_side_effects=True, vmem_limit_bytes=VMEM_LIMIT),
+    )(*(
+        pltpu.with_memory_space_constraint(x, pltpu.HBM)
+        for x in (alignment.T, seq_weight.reshape(1, -1), couplings.T, fields)
+    ))
     sums = sums.T
     row_residues = alignment.shape[1]
     column_residues = couplings.shape[1] // Q

time: 72.2 us -> 65.5 us (0.907)
  Pallas kernels: 64.9 us -> 59.9 us
  local copies, waits for them, and re-layouts: 2.04 us -> 0.7 us
    pallas_call x1, Pallas kernels: 64.9 us -> 59.9 us  [on_device(): pl.pallas_call(kernel, out_shape=(jax.ShapeDtypeStruct(couplings.shape[::...]
    reshape x1 -> x0, local copies, waits for them, and re-layouts: 1.34 us -> none  [on_device(): fields.reshape(1, -1)]
where the time goes in v3:
time: 65.5 us; the launch traced here: 65.3 us
  Pallas kernels  59.9 us (91%)
  other arithmetic  4.04 us (6%)
  local copies, waits for them, and re-layouts  0.7 us (1%)
  between operations  0.7 us (1%)
    pallas_call x1, Pallas kernels, on_device(): pl.pallas_call(kernel, out_shape=(jax.ShapeDtypeStruct(couplings.shape[::...  59.9 us
    sub x2, other arithmetic, adam_update(): return (values - change, first_new, second_new)  4.01 us

profile of v3, /device:TPU:1, one launch (start us, length us, event | category | flops | bytes accessed | tf_op | source)
XLA Modules:
  0.0 65.3 jit_solution(9105090795511082437)
XLA Ops:
  0.6 0.0 copy-start
  0.6 59.9 %shard_map.127 = (f32[315,630]{1,0:T(8,128)S(1)}, f32[1,640]{1,0:T(1,128)S(1)}) custom-call(s32[30,512]{1,0:T(8,128)} %bitcast.14, f32[1,512]{1,0:T(1,128)} %bitcast.15, f32[315,630]{1,0:T(8,128)} %bitcast.13, f32[630]{0:T(1024)} %f_in.1), custom_call_target="tpu_custom_call" | custom-call | tf_op jit(solution)/shard_map/pallas_call | solution.py:484
  60.6 0.0 copy-done
  60.6 0.0 copy-start.3
  60.6 3.4 %divide_subtract_fusion = (f32[630,315]{0,1:T(8,128)}, f32[630,315]{0,1:T(8,128)}, f32[630,315]{0,1:T(8,128)}) fusion(f32[630,315]{0,1:T(8,128)S(1)} %copy-done, f32[315,630]{1,0:T(8,128)S(1)} %get-tuple-element.8, s32[315]{0:T(512)S(1)} %fusion.7, s32[630]{0:T(1024)S(1)} %fusion.2, f32[630,315]{0,1:T(8,128)} %param.11, f32[630,315]{0,1:T(8,128)} %param.12), kind=kLoop, calls=%fused_computation.4 | loop fusion | flops 3175200 | bytes 5560380 | tf_op jit(solution)/shard_map/sub | solution.py:477
  64.0 0.0 copy-start.1
  64.0 0.0 copy-start.2
  64.0 0.0 copy-done.3
  64.0 0.7 %copy-done.1 = f32[630]{0:T(1024)S(1)} copy-done((f32[630]{0:T(1024)S(1)}, f32[630]{0:T(1024)}, u32[]{:S(2)}) %copy-start.1) | copy-done | bytes 2544
  64.7 0.0 copy-done.2
  64.7 0.6 divide_subtract_fusion.1
  (3 shorter events, 0.0 us)
Async XLA Ops:
  0.6 60.0 %copy-start = (f32[630,315]{0,1:T(8,128)S(1)}, f32[630,315]{0,1:T(8,128)}, u32[]{:S(2)}) copy-start(f32[630,315]{0,1:T(8,128)} %param.10) | copy-start | bytes 2381404
  60.6 3.4 %copy-start.3 = (f32[630]{0:T(1024)S(1)}, f32[630]{0:T(1024)}, u32[]{:S(2)}) copy-start(f32[630]{0:T(1024)} %param.15) | copy-start | bytes 7564
  64.0 0.7 %copy-start.1 = (f32[630]{0:T(1024)S(1)}, f32[630]{0:T(1024)}, u32[]{:S(2)}) copy-start(f32[630]{0:T(1024)} %f_in.1) | copy-start | bytes 7564
  64.0 0.7 %copy-start.2 = (f32[630]{0:T(1024)S(1)}, f32[630]{0:T(1024)}, u32[]{:S(2)}) copy-start(f32[630]{0:T(1024)} %param.14) | copy-start | bytes 7564

commit v4 on v3

--- a/solution.py
+++ b/solution.py
@@ -11,7 +11,7 @@
 F32 = jnp.float32
 BF16 = jnp.bfloat16
 VMEM_LIMIT = 24 * 2**20
-ROW_GROUPS = ((0, 384), (384, 640))
+ROW_GROUPS = ((0, 256), (256, 512), (512, 640))
 
 
 def two_parts(x):
@@ -65,6 +65,23 @@
 
 def far(i):
     return (i + 2) % 4
+
+
+def spread_lanes(x):
+    at = iota((1, 128), 1)
+    tiles = [x[:, 0:128]]
+    for t in range(1, 5):
+        last, this = x[:, 128 * t - 128 : 128 * t], x[:, 128 * t : 128 * t + 128]
+        tiles.append(jnp.where(at < 2 * t, pltpu.roll(last, 2 * t, 1), pltpu.roll(this, 2 * t, 1)))
+    return jnp.concatenate(tiles, axis=1)
+
+
+def natural_tile(tile, t):
+    at = iota((1, 128), 1)
+    this = tile(t) if t == 0 else pltpu.roll(tile(t), 128 - 2 * t, 1)
+    if t == 4:
+        return this
+    return jnp.where(at < 126 - 2 * t, this, pltpu.roll(tile(t + 1), 126 - 2 * t, 1))
 
 
 class Reduce:
@@ -130,30 +147,31 @@
     def blocks(self):
         return [(h, i) for h in range(2) for i in (self.b, order(self.b, h)[1])]
 
-    def result(self):
-        for sent in self.s4.values():
-            for copy in sent:
+    def result(self, g):
+        at = self.lanes(g)
+        for h in range(2):
+            for copy in self.s4[g, h]:
                 copy.wait_recv()
         parts = [
-            self.total[self.a, h, i] + self.ins[3][h, n % 2] for n, (h, i) in enumerate(self.blocks())
+            self.total[self.a, h, i, :, at] + self.ins[3][h, n % 2, :, at]
+            for n, (h, i) in enumerate(self.blocks())
         ]
         return jnp.concatenate(parts, axis=0)
 
-    def gather1(self, value):
+    def gather1(self, g, value):
+        at = self.lanes(g)
         for n, (h, i) in enumerate(self.blocks()):
-            self.full[self.a, h, i] = value[8 * n : 8 * n + 8]
-        for g in range(len(self.groups)):
-            at = self.lanes(g)
-            for h in range(2):
-                p, q = order(self.b, h)
-                self.g1[g, h] = [
-                    self.exchange(
-                        self.full.at[self.a, h, i, :, at],
-                        self.full.at[self.a, h, i, :, at],
-                        self.at(self.a, p),
-                    )
-                    for i in (self.b, q)
-                ]
+            self.full[self.a, h, i, :, at] = value[8 * n : 8 * n + 8]
+        for h in range(2):
+            p, q = order(self.b, h)
+            self.g1[g, h] = [
+                self.exchange(
+                    self.full.at[self.a, h, i, :, at],
+                    self.full.at[self.a, h, i, :, at],
+                    self.at(self.a, p),
+                )
+                for i in (self.b, q)
+            ]
 
     def gather2(self, g):
         at = self.lanes(g)
@@ -180,10 +198,10 @@
 
 
 def kernel(
-    al_in, w_in, j_ref, f_in, g_ref, fg_ref,
-    states, oc32, or32, oct, j_high, j_low, j_in, xr, xc,
+    al_in, w_in, j_ref, f_in, fm_in, fs_in, g_ref, nf_ref, nfm_ref, nfs_ref,
+    states, oc32, or32, oct, j_pad, j_high, j_low, j_in, xr, xc,
     r_in1, r_in2, r_in3, r_in4, c_in1, c_in2, c_in3, c_in4, wr, wc, acc,
-    fpad, al_ref, w_ref, j_own, f_ref, local, state_send, send, recv,
+    fpad, fg_ref, al_ref, w_ref, j_own, f_ref, fm_ref, fs_ref, local, state_send, send, recv,
 ):
     row, col = lax.axis_index("row"), lax.axis_index("col")
     z_lo, x = row // 4, row % 4
@@ -208,7 +226,7 @@
     loads = [
         pltpu.make_async_copy(src, dst, local.at[n])
         for n, (src, dst) in enumerate(
-            ((al_in, al_ref), (f_in, f_ref), (j_ref, j_own), (w_in, w_ref))
+            ((al_in, al_ref), (f_in, f_ref), (j_ref, j_own), (w_in, w_ref), (fm_in, fm_ref), (fs_in, fs_ref))
         )
     ]
     for load in loads:
@@ -217,6 +235,7 @@
     loads[1].wait()
 
     fpad[...] = jnp.zeros_like(fpad)
+    fg_ref[...] = jnp.zeros_like(fg_ref)
     fpad[0:1, 0:630] = f_ref[...].reshape(1, 630)
     fields = fpad[...]
     field_lane = iota((8, 640), 1)
@@ -232,6 +251,31 @@
     word_line = iota((8, 512), 0)
     words = jnp.where(word_line == 6, fields0, jnp.where(word_line == 7, fields1, words))
 
+    loads[2].wait()
+    for load in loads[3:]:
+        load.wait()
+    j_pad[...] = jnp.zeros_like(j_pad)
+    j_pad[0:315, 0:630] = j_own[...]
+    high, low = two_parts(spread_lanes(j_pad[...]))
+    j_high[0:320, :] = high
+    j_low[0:320, :] = low
+
+    lane_r = iota((1, 640), 1)
+
+    def tile_residue(lane):
+        tile = lane // 128
+        return tile * 6 + residue_of(lane - tile * 128)
+
+    inside = lane_r % 128 < 126
+    res_r = jnp.where(inside, tile_residue(lane_r), -1)
+    state_r = (lane_r % 128) - residue_of(lane_r % 128) * Q
+    spread_r = iota((30, 640), 0) == tile_residue(iota((30, 640), 1))
+    value_r = dot(alignment, as_bf16(spread_r), ((0,), (0,)))
+    hot_r = (value_r == state_r.astype(F32)) & inside
+    hot_r = hot_r.astype(F32)
+    or32[...] = hot_r.reshape(64, 8, 640)
+    hot_r = hot_r.astype(BF16)
+
     pl.semaphore_wait(barrier, len(greeted))
 
     state_copies = [
@@ -260,23 +304,6 @@
         return copy
 
     across = exchange(j_ref, j_in, partner)
-    j_high[...] = jnp.zeros_like(j_high)
-    j_low[...] = jnp.zeros_like(j_low)
-    loads[2].wait()
-    loads[3].wait()
-    high, low = two_parts(j_own[...])
-    j_high[0:315, 0:630] = high
-    j_low[0:315, 0:630] = low
-
-    lane_r = iota((1, 640), 1)
-    res_r = residue_of(lane_r)
-    spread_r = iota((30, 640), 0) == residue_of(iota((30, 640), 1))
-    value_r = dot(alignment, as_bf16(spread_r), ((0,), (0,)))
-    hot_r = (value_r == (lane_r - res_r * Q).astype(F32)) & (lane_r < 630)
-    hot_r = hot_r.astype(F32)
-    or32[...] = hot_r.reshape(64, 8, 640)
-    hot_r = hot_r.astype(BF16)
-
     nt = ((1,), (1,))
     top, bottom = hot_r[0:256], hot_r[256:512]
     none = jnp.zeros((64, 640), BF16)
@@ -300,9 +327,10 @@
     cols.step1(0)
 
     across.wait_recv()
-    high, low = two_parts(j_in[...])
-    j_high[320:635, 0:630] = high
-    j_low[320:635, 0:630] = low
+    j_pad[0:315, 0:630] = j_in[...]
+    high, low = two_parts(spread_lanes(j_pad[...]))
+    j_high[320:640, :] = high
+    j_low[320:640, :] = low
 
     @pl.when(row != owner)
     def _():
@@ -370,7 +398,7 @@
         return jnp.sum(jnp.concatenate(found, axis=0), axis=1, keepdims=True)
 
     def residual(energy, hot, residue, weight):
-        member = as_bf16(iota((128, 640), 0) == residue)
+        member = as_bf16(iota((128, energy.shape[1]), 0) == residue)
         powers = jnp.exp(energy)
         lines = energy.shape[0]
         parts = dot(jnp.concatenate(three_parts(powers), axis=0), member, nt)
@@ -398,16 +426,20 @@
     f_tail = (f_tail + pltpu.roll(f_tail, 64, 1))[0:1]
     fields_c = jnp.concatenate([f_main, f_main, f_tail], axis=1)
     weight = jnp.where(second, line_weights(first + 256), line_weights(first))
-    cols.gather1(residual(cols.result() + fields_c, hot, residue_c, weight))
-    cols.gather2(0)
-
-    residue_rows = jnp.where(lane_r < 630, res_r, -1)
+    cols.gather1(0, residual(cols.result(0) + fields_c, hot, residue_c, weight))
+
     block = core * 32 + y * 8
-    hot = jnp.concatenate([or32[block + 4 * h + i] for h, i in rows.blocks()], axis=0)
     first_blocks = rows.blocks()
     weight = line_weights(core * 256 + y * 64)
-    rows.gather1(residual(rows.result() + fpad[0:1, :], hot, residue_rows, weight))
-
+    fields_r = spread_lanes(fpad[...])[0:1]
+    for g in row_groups:
+        low, high = ROW_GROUPS[g]
+        at = rows.lanes(g)
+        hot = jnp.concatenate([or32[block + 4 * h + i, :, at] for h, i in rows.blocks()], axis=0)
+        energy = rows.result(g) + fields_r[:, low:high]
+        rows.gather1(g, residual(energy, hot, res_r[:, low:high], weight))
+        if g == 0:
+            cols.gather2(0)
     cols.gather3(0)
     for g in row_groups:
         rows.gather2(g)
@@ -426,11 +458,11 @@
         return sum(dot(piece, hot, ((0,), (0,))) for piece in two_parts(lines))
 
     acc[...] = products(0, first_c)
-    last = []
+    last = {g: [] for g in row_groups}
 
     def forward(i, h, g):
         piece = wr.at[core, i, h, :, :, rows.lanes(g)]
-        last.append(exchange(piece, piece, partner))
+        last[g].append(exchange(piece, piece, partner))
 
     for g in row_groups:
         rows.gather3(g)
@@ -444,20 +476,36 @@
             forward(order(y, h)[0], h, g)
             forward(far(y), h, g)
 
-    def row_products(which):
-        lines = wr[which].reshape(256, 640)
+    def row_products(which, g):
+        lines = wr[which, :, :, :, :, rows.lanes(g)].reshape(256, -1)
         hot = oct[which]
-        sums = sum(dot(hot, piece) for piece in two_parts(lines))
-        return sums, jnp.sum(lines, axis=0, keepdims=True)
-
-    sums, line_sum = row_products(core)
-    acc[0:320, :] += sums
-    for copy in last:
-        copy.wait_recv()
-    sums, other_sum = row_products(1 - core)
-    fg_ref[...] = line_sum + other_sum
-    total = acc[0:320, :] + sums
-    g_ref[...] = total[0:315, 0:630]
+        acc[0:320, rows.lanes(g)] += sum(dot(hot, piece) for piece in two_parts(lines))
+        return jnp.sum(lines, axis=0, keepdims=True)
+
+    def finish(t):
+        high = min(128 * t + 128, 630)
+        tile = natural_tile(lambda i: acc[0:320, 128 * i : 128 * i + 128], t)
+        g_ref[:, 128 * t : high] = tile[0:315, 0 : high - 128 * t]
+
+    line_sums = [row_products(core, g) for g in row_groups]
+    done = 0
+    for g in row_groups:
+        for copy in last[g]:
+            copy.wait_recv()
+        fg_ref[0:1, rows.lanes(g)] = line_sums[g] + row_products(1 - core, g)
+        ready = ROW_GROUPS[g][1] // 128
+        for t in range(done, ready - (ready < 5)):
+            finish(t)
+        done = ready - 1
+
+    def grad_tile(i):
+        return fg_ref[:, 128 * i : 128 * i + 128]
+
+    grad = jnp.concatenate([natural_tile(grad_tile, t) for t in range(5)], axis=1)[0:1, 0:630]
+    moments = (f_ref, fm_ref, fs_ref)
+    new = adam_update(*(ref[...].reshape(1, 630) for ref in moments), grad)
+    for ref, value in zip((nf_ref, nfm_ref, nfs_ref), new):
+        ref[...] = value.reshape(630)
 
     for copy in copies:
         copy.wait_send()
@@ -471,9 +519,8 @@
 def adam_update(values, first_moment, second_moment, gradient):
     first_new = 0.9 * first_moment + 0.1 * gradient
     second_new = 0.999 * second_moment + 0.001 * gradient * gradient
-    change = (
-        0.05 * (first_new / (1.0 - 0.9**10)) / (jnp.sqrt(second_new / (1.0 - 0.999**10)) + 1e-08)
-    )
+    root = jnp.sqrt(second_new * (1.0 / (1.0 - 0.999**10)))
+    change = first_new * (0.05 / (1.0 - 0.9**10)) / (root + 1e-08)
     return (values - change, first_new, second_new)
 
 
@@ -481,19 +528,20 @@
     alignment, seq_weight, couplings, pair_mean, pair_square, fields, field_mean, field_square
 ):
     vmem = pl.BlockSpec(memory_space=pltpu.VMEM)
-    sums, field_sums = pl.pallas_call(
+    sums, new_fields, new_field_mean, new_field_square = pl.pallas_call(
         kernel,
         out_shape=(
             jax.ShapeDtypeStruct(couplings.shape[::-1], F32),
-            jax.ShapeDtypeStruct((1, 640), F32),
+            *[jax.ShapeDtypeStruct(fields.shape, F32)] * 3,
         ),
-        in_specs=[pl.BlockSpec(memory_space=pltpu.HBM)] * 4,
-        out_specs=(vmem, vmem),
+        in_specs=[pl.BlockSpec(memory_space=pltpu.HBM)] * 6,
+        out_specs=(vmem,) * 4,
         scratch_shapes=[
             pltpu.VMEM((8, 512), F32),
             pltpu.VMEM((64, 8, 384), F32),
             pltpu.VMEM((64, 8, 640), F32),
             pltpu.VMEM((2, 320, 256), BF16),
+            pltpu.VMEM((320, 640), F32),
             pltpu.VMEM((640, 640), BF16),
             pltpu.VMEM((640, 640), BF16),
             pltpu.VMEM(couplings.shape[::-1], F32),
@@ -510,19 +558,20 @@
             pltpu.VMEM((4, 2, 4, 8, 640), F32),
             pltpu.VMEM((384, 640), F32),
             pltpu.VMEM((8, 640), F32),
+            pltpu.VMEM((8, 640), F32),
             pltpu.VMEM(alignment.shape[::-1], jnp.int32),
             pltpu.VMEM((1, 512), F32),
             pltpu.VMEM(couplings.shape[::-1], F32),
-            pltpu.VMEM(fields.shape, F32),
-            pltpu.SemaphoreType.DMA((4,)),
+            *[pltpu.VMEM(fields.shape, F32)] * 3,
+            pltpu.SemaphoreType.DMA((6,)),
             pltpu.SemaphoreType.DMA((16,)),
-            pltpu.SemaphoreType.DMA((96,)),
-            pltpu.SemaphoreType.DMA((96,)),
+            pltpu.SemaphoreType.DMA((136,)),
+            pltpu.SemaphoreType.DMA((136,)),
         ],
         compiler_params=pltpu.CompilerParams(collective_id=0, has_side_effects=True, vmem_limit_bytes=VMEM_LIMIT),
     )(*(
         pltpu.with_memory_space_constraint(x, pltpu.HBM)
-        for x in (alignment.T, seq_weight.reshape(1, -1), couplings.T, fields)
+        for x in (alignment.T, seq_weight.reshape(1, -1), couplings.T, fields, field_mean, field_square)
     ))
     sums = sums.T
     row_residues = alignment.shape[1]
@@ -536,12 +585,8 @@
         + lax.broadcasted_iota(jnp.int32, (1, couplings.shape[1]), 1) // Q
     )
     pair_grad = jnp.where(row_ids != column_ids, sums, 0.0) + 0.2 * (L - 1) * couplings
-    field_grad = field_sums[0, : fields.shape[0]]
     new_pairs, new_pair_mean, new_pair_square = adam_update(
         couplings, pair_mean, pair_square, pair_grad
-    )
-    new_fields, new_field_mean, new_field_square = adam_update(
-        fields, field_mean, field_square, field_grad
     )
     return (new_pairs, new_pair_mean, new_pair_square, new_fields, new_field_mean, new_field_square)
 

time: 65.5 us -> 65.9 us (level)
  local copies, waits for them, and re-layouts: 0.7 us -> 1.79 us
  other arithmetic: 4.04 us -> 3.38 us
    unnamed x8 -> x5, local copies, waits for them, and re-layouts: 0.69 us -> 1.79 us
    sub x2 -> x1, other arithmetic: 4.01 us -> 3.35 us  [adam_update(): return (values - change, first_new, second_new)]
where the time goes in v4:
time: 65.9 us; the launch traced here: 65.8 us
  Pallas kernels  59.9 us (91%)
  other arithmetic  3.38 us (5%)
  local copies, waits for them, and re-layouts  1.79 us (3%)
  between operations  0.67 us (1%)
    pallas_call x1, Pallas kernels, on_device(): pl.pallas_call(kernel, out_shape=(jax.ShapeDtypeStruct(couplings.shape[::...  59.9 us
    sub x1, other arithmetic, adam_update(): return (values - change, first_new, second_new)  3.35 us
    unnamed x5, local copies, waits for them, and re-layouts  1.79 us

profile of v4, /device:TPU:1, one launch (start us, length us, event | category | flops | bytes accessed | tf_op | source)
XLA Modules:
  0.0 65.8 jit_solution(12044785758287424450)
XLA Ops:
  0.6 0.0 copy-start
  0.7 59.9 %shard_map.127 = (f32[315,630]{1,0:T(8,128)S(1)}, f32[630]{0:T(1024)S(1)}, f32[630]{0:T(1024)S(1)}, f32[630]{0:T(1024)S(1)}) custom-call(s32[30,512]{1,0:T(8,128)} %bitcast.14, f32[1,512]{1,0:T(1,128)} %bitcast.15, f32[315,630]{1,0:T(8,128)} %bitcast.13, f32[630]{0:T(1024)} %f_in.1, f32[630]{0:T(1024)} %fm_in.1, f32[630]{0:T(1024)} %fs_in.1), custom_call_target="tpu_custom_call" | custom-call | tf_op jit(solution)/shard_map/pallas_call | solution.py:531
  60.6 0.0 copy-done
  60.6 3.4 %divide_subtract_fusion = (f32[630,315]{0,1:T(8,128)}, f32[630,315]{0,1:T(8,128)}, f32[630,315]{0,1:T(8,128)}) fusion(f32[630,315]{0,1:T(8,128)S(1)} %copy-done, f32[315,630]{1,0:T(8,128)S(1)} %get-tuple-element.10, s32[315]{0:T(512)S(1)} %fusion.6, s32[630]{0:T(1024)S(1)} %fusion.2, f32[630,315]{0,1:T(8,128)} %param.11, f32[630,315]{0,1:T(8,128)} %param.12), kind=kLoop, calls=%fused_computation.4 | loop fusion | flops 3175200 | bytes 5560380 | tf_op jit(solution)/shard_map/sub | solution.py:524
  64.0 0.6 copy.17
  64.6 0.6 copy.18
  65.2 0.6 copy.19
  (2 shorter events, 0.0 us)
Async XLA Ops:
  0.6 60.0 %copy-start = (f32[630,315]{0,1:T(8,128)S(1)}, f32[630,315]{0,1:T(8,128)}, u32[]{:S(2)}) copy-start(f32[630,315]{0,1:T(8,128)} %param.10) | copy-start | bytes 2381404

commit v5 on v4

--- a/solution.py
+++ b/solution.py
@@ -11,6 +11,7 @@
 F32 = jnp.float32
 BF16 = jnp.bfloat16
 VMEM_LIMIT = 24 * 2**20
+SENDS = 40
 ROW_GROUPS = ((0, 256), (256, 512), (512, 640))
 
 
@@ -85,62 +86,54 @@
 
 
 class Reduce:
-    def __init__(self, exchange, a, b, at, total, ins, full, groups):
+    def __init__(self, exchange, a, b, at, total, ins, full):
         self.exchange, self.a, self.b, self.at = exchange, a, b, at
-        self.total, self.ins, self.full, self.groups = total, ins, full, groups
+        self.total, self.ins, self.full = total, ins, full
         self.s1, self.s2, self.s3, self.s4 = {}, {}, {}, {}
         self.g1, self.g2, self.g3 = {}, {}, {}
 
-    def lanes(self, g):
-        low, high = self.groups[g]
-        return pl.ds(low, high - low)
-
     def step1(self, g):
-        at = self.lanes(g)
         for h in range(2):
             p, _ = order(self.a, h)
             to = self.at(p, self.b)
-            later = self.total.at[far(self.a), h, :, :, at]
-            theirs = self.total.at[p, h, :, :, at]
-            one = self.exchange(later, self.ins[0].at[h, 1, :, :, at], to)
-            two = self.exchange(theirs, self.ins[0].at[h, 0, :, :, at], to)
+            later = self.total[g].at[far(self.a), h]
+            theirs = self.total[g].at[p, h]
+            one = self.exchange(later, self.ins[0][g].at[h, 1], to)
+            two = self.exchange(theirs, self.ins[0][g].at[h, 0], to)
             self.s1[g, h] = (two, one)
 
     def step2(self, g):
-        at = self.lanes(g)
         for h in range(2):
             p, q = order(self.a, h)
             self.s1[g, h][1].wait_recv()
-            self.total[q, h, :, :, at] += self.ins[0][h, 1, :, :, at]
+            self.total[g][q, h] += self.ins[0][g][h, 1]
             self.s2[g, h] = self.exchange(
-                self.total.at[q, h, :, :, at], self.ins[1].at[h, :, :, at], self.at(q, self.b)
+                self.total[g].at[q, h], self.ins[1][g].at[h], self.at(q, self.b)
             )
         for h in range(2):
             self.s1[g, h][0].wait_recv()
-            self.total[self.a, h, :, :, at] += self.ins[0][h, 0, :, :, at]
+            self.total[g][self.a, h] += self.ins[0][g][h, 0]
 
     def step3(self, g):
-        at = self.lanes(g)
         for h in range(2):
             p, _ = order(self.b, h)
             self.s2[g, h].wait_recv()
-            self.total[self.a, h, :, :, at] += self.ins[1][h, :, :, at]
+            self.total[g][self.a, h] += self.ins[1][g][h]
             to = self.at(self.a, p)
             self.s3[g, h] = [
-                self.exchange(self.total.at[self.a, h, i, :, at], self.ins[2].at[h, n, :, at], to)
+                self.exchange(self.total[g].at[self.a, h, i], self.ins[2][g].at[h, n], to)
                 for n, i in enumerate((p, far(self.b)))
             ]
 
     def step4(self, g):
-        at = self.lanes(g)
         for h in range(2):
             p, q = order(self.b, h)
             to = self.at(self.a, q)
             for n, i in enumerate((self.b, q)):
                 self.s3[g, h][n].wait_recv()
-                self.total[self.a, h, i, :, at] += self.ins[2][h, n, :, at]
+                self.total[g][self.a, h, i] += self.ins[2][g][h, n]
             self.s4[g, h] = [
-                self.exchange(self.total.at[self.a, h, i, :, at], self.ins[3].at[h, 1 - n, :, at], to)
+                self.exchange(self.total[g].at[self.a, h, i], self.ins[3][g].at[h, 1 - n], to)
                 for n, i in enumerate((self.b, q))
             ]
 
@@ -148,46 +141,42 @@
         return [(h, i) for h in range(2) for i in (self.b, order(self.b, h)[1])]
 
     def result(self, g):
-        at = self.lanes(g)
         for h in range(2):
             for copy in self.s4[g, h]:
                 copy.wait_recv()
         parts = [
-            self.total[self.a, h, i, :, at] + self.ins[3][h, n % 2, :, at]
+            self.total[g][self.a, h, i] + self.ins[3][g][h, n % 2]
             for n, (h, i) in enumerate(self.blocks())
         ]
         return jnp.concatenate(parts, axis=0)
 
     def gather1(self, g, value):
-        at = self.lanes(g)
         for n, (h, i) in enumerate(self.blocks()):
-            self.full[self.a, h, i, :, at] = value[8 * n : 8 * n + 8]
+            self.full[g][self.a, h, i] = value[8 * n : 8 * n + 8]
         for h in range(2):
             p, q = order(self.b, h)
             self.g1[g, h] = [
                 self.exchange(
-                    self.full.at[self.a, h, i, :, at],
-                    self.full.at[self.a, h, i, :, at],
+                    self.full[g].at[self.a, h, i],
+                    self.full[g].at[self.a, h, i],
                     self.at(self.a, p),
                 )
                 for i in (self.b, q)
             ]
 
     def gather2(self, g):
-        at = self.lanes(g)
         for h in range(2):
             p, q = order(self.a, h)
             for copy in self.g1[g, h]:
                 copy.wait_recv()
-            own = self.full.at[self.a, h, :, :, at]
+            own = self.full[g].at[self.a, h]
             self.g2[g, h] = self.exchange(own, own, self.at(q, self.b))
             self.g3[g, h] = [self.exchange(own, own, self.at(p, self.b))]
 
     def gather3(self, g):
-        at = self.lanes(g)
         for h in range(2):
             p, q = order(self.a, h)
-            second = self.full.at[q, h, :, :, at]
+            second = self.full[g].at[q, h]
             self.g2[g, h].wait_recv()
             self.g3[g, h].append(self.exchange(second, second, self.at(p, self.b)))
 
@@ -198,7 +187,7 @@
 
 
 def kernel(
-    al_in, w_in, j_ref, f_in, fm_in, fs_in, g_ref, nf_ref, nfm_ref, nfs_ref,
+    al_in, w_in, j_ref, f_in, fm_in, fs_in, g_ref, field_ref,
     states, oc32, or32, oct, j_pad, j_high, j_low, j_in, xr, xc,
     r_in1, r_in2, r_in3, r_in4, c_in1, c_in2, c_in3, c_in4, wr, wc, acc,
     fpad, fg_ref, al_ref, w_ref, j_own, f_ref, fm_ref, fs_ref, local, state_send, send, recv,
@@ -216,13 +205,6 @@
 
     partner = (row, y * 8 + z_hi * 2 + 1 - core)
 
-    barrier = pltpu.get_barrier_semaphore()
-    greeted = [at_row(flip(y), z_hi), at_row(mirror(y), z_hi), at_row(y, flip(z_hi))]
-    greeted += [at_row(y, mirror(z_hi)), partner]
-    greeted += [((row + d) % 16, col) for d in range(1, 16)]
-    for device in greeted:
-        pl.semaphore_signal(barrier, inc=1, device_id=device, device_id_type=MESH)
-
     loads = [
         pltpu.make_async_copy(src, dst, local.at[n])
         for n, (src, dst) in enumerate(
@@ -231,6 +213,14 @@
     ]
     for load in loads:
         load.start()
+
+    barrier = pltpu.get_barrier_semaphore()
+    greeted = [at_row(flip(y), z_hi), at_row(mirror(y), z_hi), at_row(y, flip(z_hi))]
+    greeted += [at_row(y, mirror(z_hi)), partner]
+    greeted += [((row + d) % 16, col) for d in range(1, 16)]
+    for device in greeted:
+        pl.semaphore_signal(barrier, inc=1, device_id=device, device_id_type=MESH)
+
     loads[0].wait()
     loads[1].wait()
 
@@ -295,9 +285,11 @@
     copies = []
 
     def exchange(src, dst, device):
-        at = len(copies) + 1
+        at = len(copies)
+        if at >= SENDS:
+            copies[at - SENDS].wait_send()
         copy = pltpu.make_async_remote_copy(
-            src, dst, send.at[at], recv.at[at], device_id=device, device_id_type=MESH
+            src, dst, send.at[at % SENDS], recv.at[at + 1], device_id=device, device_id_type=MESH
         )
         copy.start()
         copies.append(copy)
@@ -318,12 +310,16 @@
     ).reshape(4, 2, 4, 8, 128)
 
     cols = Reduce(
-        exchange, x, z_lo, at_col, xc, (c_in1, c_in2, c_in3, c_in4), wc, ((0, 640),)
+        exchange, x, z_lo, at_col, [xc], ([c_in1], [c_in2], [c_in3], [c_in4]), [wc]
     )
     rows = Reduce(
-        exchange, y, z_hi, at_row, xr, (r_in1, r_in2, r_in3, r_in4), wr.at[core], ROW_GROUPS
+        exchange, y, z_hi, at_row, xr, (r_in1, r_in2, r_in3, r_in4), [w.at[core] for w in wr]
     )
     row_groups = range(len(ROW_GROUPS))
+
+    def lanes(g):
+        return slice(*ROW_GROUPS[g])
+
     cols.step1(0)
 
     across.wait_recv()
@@ -363,9 +359,9 @@
     hot_b = (value_b == (local - residue_of(local) * Q).astype(F32)) & (local < 315)
     hot_b = as_bf16(hot_b)
     for g in row_groups:
-        at = rows.lanes(g)
+        at = lanes(g)
         sums = dot(hot_b, j_high[:, at]) + dot(hot_b, j_low[:, at])
-        xr[:, :, :, :, at] = sums.reshape(4, 2, 4, 8, -1)
+        xr[g][...] = sums.reshape(4, 2, 4, 8, -1)
         rows.step1(g)
 
     lane_c = iota((1, 384), 1)
@@ -434,7 +430,7 @@
     fields_r = spread_lanes(fpad[...])[0:1]
     for g in row_groups:
         low, high = ROW_GROUPS[g]
-        at = rows.lanes(g)
+        at = lanes(g)
         hot = jnp.concatenate([or32[block + 4 * h + i, :, at] for h, i in rows.blocks()], axis=0)
         energy = rows.result(g) + fields_r[:, low:high]
         rows.gather1(g, residual(energy, hot, res_r[:, low:high], weight))
@@ -461,7 +457,7 @@
     last = {g: [] for g in row_groups}
 
     def forward(i, h, g):
-        piece = wr.at[core, i, h, :, :, rows.lanes(g)]
+        piece = wr[g].at[core, i, h]
         last[g].append(exchange(piece, piece, partner))
 
     for g in row_groups:
@@ -476,10 +472,13 @@
             forward(order(y, h)[0], h, g)
             forward(far(y), h, g)
 
+    for n, ref in enumerate((f_ref, fm_ref, fs_ref)):
+        field_ref[n : n + 1, 0:630] = ref[...].reshape(1, 630)
+
     def row_products(which, g):
-        lines = wr[which, :, :, :, :, rows.lanes(g)].reshape(256, -1)
+        lines = wr[g][which].reshape(256, -1)
         hot = oct[which]
-        acc[0:320, rows.lanes(g)] += sum(dot(hot, piece) for piece in two_parts(lines))
+        acc[0:320, lanes(g)] += sum(dot(hot, piece) for piece in two_parts(lines))
         return jnp.sum(lines, axis=0, keepdims=True)
 
     def finish(t):
@@ -492,7 +491,7 @@
     for g in row_groups:
         for copy in last[g]:
             copy.wait_recv()
-        fg_ref[0:1, rows.lanes(g)] = line_sums[g] + row_products(1 - core, g)
+        fg_ref[0:1, lanes(g)] = line_sums[g] + row_products(1 - core, g)
         ready = ROW_GROUPS[g][1] // 128
         for t in range(done, ready - (ready < 5)):
             finish(t)
@@ -501,13 +500,10 @@
     def grad_tile(i):
         return fg_ref[:, 128 * i : 128 * i + 128]
 
-    grad = jnp.concatenate([natural_tile(grad_tile, t) for t in range(5)], axis=1)[0:1, 0:630]
-    moments = (f_ref, fm_ref, fs_ref)
-    new = adam_update(*(ref[...].reshape(1, 630) for ref in moments), grad)
-    for ref, value in zip((nf_ref, nfm_ref, nfs_ref), new):
-        ref[...] = value.reshape(630)
-
-    for copy in copies:
+    grad = jnp.concatenate([natural_tile(grad_tile, t) for t in range(5)], axis=1)
+    field_ref[3:4, :] = grad[0:1]
+
+    for copy in copies[-SENDS:]:
         copy.wait_send()
 
     @pl.when(row == owner)
@@ -528,14 +524,18 @@
     alignment, seq_weight, couplings, pair_mean, pair_square, fields, field_mean, field_square
 ):
     vmem = pl.BlockSpec(memory_space=pltpu.VMEM)
-    sums, new_fields, new_field_mean, new_field_square = pl.pallas_call(
+
+    def by_group(*dims):
+        return [pltpu.VMEM((*dims, high - low), F32) for low, high in ROW_GROUPS]
+
+    sums, field_lines = pl.pallas_call(
         kernel,
         out_shape=(
             jax.ShapeDtypeStruct(couplings.shape[::-1], F32),
-            *[jax.ShapeDtypeStruct(fields.shape, F32)] * 3,
+            jax.ShapeDtypeStruct((4, 640), F32),
         ),
         in_specs=[pl.BlockSpec(memory_space=pltpu.HBM)] * 6,
-        out_specs=(vmem,) * 4,
+        out_specs=(vmem, vmem),
         scratch_shapes=[
             pltpu.VMEM((8, 512), F32),
             pltpu.VMEM((64, 8, 384), F32),
@@ -546,15 +546,14 @@
             pltpu.VMEM((640, 640), BF16),
             pltpu.VMEM(couplings.shape[::-1], F32),
         ]
-        + [pltpu.VMEM((4, 2, 4, 8, 640), F32)] * 2
+        + [by_group(4, 2, 4, 8), pltpu.VMEM((4, 2, 4, 8, 640), F32)]
+        + [by_group(2, 2, 4, 8), by_group(2, 4, 8), by_group(2, 2, 8), by_group(2, 2, 8)]
         + [
             pltpu.VMEM((2, 2, 4, 8, 640), F32),
             pltpu.VMEM((2, 4, 8, 640), F32),
             pltpu.VMEM((2, 2, 8, 640), F32),
             pltpu.VMEM((2, 2, 8, 640), F32),
-        ] * 2
-        + [
-            pltpu.VMEM((2, 4, 2, 4, 8, 640), F32),
+            by_group(2, 4, 2, 4, 8),
             pltpu.VMEM((4, 2, 4, 8, 640), F32),
             pltpu.VMEM((384, 640), F32),
             pltpu.VMEM((8, 640), F32),
@@ -565,8 +564,8 @@
             *[pltpu.VMEM(fields.shape, F32)] * 3,
             pltpu.SemaphoreType.DMA((6,)),
             pltpu.SemaphoreType.DMA((16,)),
-            pltpu.SemaphoreType.DMA((136,)),
-            pltpu.SemaphoreType.DMA((136,)),
+            pltpu.SemaphoreType.DMA((SENDS,)),
+            pltpu.SemaphoreType.DMA((26 + 32 * len(ROW_GROUPS),)),
         ],
         compiler_params=pltpu.CompilerParams(collective_id=0, has_side_effects=True, vmem_limit_bytes=VMEM_LIMIT),
     )(*(
@@ -588,6 +587,9 @@
     new_pairs, new_pair_mean, new_pair_square = adam_update(
         couplings, pair_mean, pair_square, pair_grad
     )
+    new_fields, new_field_mean, new_field_square = adam_update(
+        *(field_lines[n, : fields.shape[0]] for n in range(4))
+    )
     return (new_pairs, new_pair_mean, new_pair_square, new_fields, new_field_mean, new_field_square)
 
 

time: 65.9 us -> 63.8 us (0.968)
  local copies, waits for them, and re-layouts: 1.79 us -> 0.01 us
  Pallas kernels: 59.9 us -> 58.8 us
  other arithmetic: 3.38 us -> 4.07 us
    unnamed x5 -> x2, local copies, waits for them, and re-layouts: 1.79 us -> 0.01 us
    pallas_call x1, Pallas kernels: 59.9 us -> 58.8 us  [on_device(): pl.pallas_call(kernel, out_shape=(jax.ShapeDtypeStruct(couplings.shape[::...]
    sub x1 -> x2, other arithmetic: 3.35 us -> 4.01 us  [adam_update(): return (values - change, first_new, second_new)]
where the time goes in v5:
time: 63.8 us; the launch traced here: 63.6 us
  Pallas kernels  58.8 us (92%)
  other arithmetic  4.07 us (6%)
  between operations  0.68 us (1%)
    pallas_call x1, Pallas kernels, on_device(): pl.pallas_call(kernel, out_shape=(jax.ShapeDtypeStruct(couplings.shape[::...  58.8 us
    sub x2, other arithmetic, adam_update(): return (values - change, first_new, second_new)  4.01 us

profile of v5, /device:TPU:1, one launch (start us, length us, event | category | flops | bytes accessed | tf_op | source)
XLA Modules:
  0.0 63.6 jit_solution(13944575083016746351)
XLA Ops:
  0.6 0.0 copy-start
  0.6 58.8 %shard_map.127 = (f32[315,630]{1,0:T(8,128)S(1)}, f32[4,640]{1,0:T(4,128)S(1)}) custom-call(s32[30,512]{1,0:T(8,128)} %bitcast.14, f32[1,512]{1,0:T(1,128)} %bitcast.15, f32[315,630]{1,0:T(8,128)} %bitcast.13, f32[630]{0:T(1024)} %f_in.1, f32[630]{0:T(1024)} %fm_in.1, f32[630]{0:T(1024)} %fs_in.1), custom_call_target="tpu_custom_call" | custom-call | tf_op jit(solution)/shard_map/pallas_call | solution.py:531
  59.5 0.0 copy-done
  59.5 3.4 %divide_subtract_fusion = (f32[630,315]{0,1:T(8,128)}, f32[630,315]{0,1:T(8,128)}, f32[630,315]{0,1:T(8,128)}) fusion(f32[630,315]{0,1:T(8,128)S(1)} %copy-done, f32[315,630]{1,0:T(8,128)S(1)} %get-tuple-element.8, s32[315]{0:T(512)S(1)} %fusion.7, s32[630]{0:T(1024)S(1)} %fusion.2, f32[630,315]{0,1:T(8,128)} %param.11, f32[630,315]{0,1:T(8,128)} %param.12), kind=kLoop, calls=%fused_computation.4 | loop fusion | flops 3175200 | bytes 5560380 | tf_op jit(solution)/shard_map/sub | solution.py:520
  63.0 0.6 divide_subtract_fusion.1
  (3 shorter events, 0.1 us)
Async XLA Ops:
  0.6 58.9 %copy-start = (f32[630,315]{0,1:T(8,128)S(1)}, f32[630,315]{0,1:T(8,128)}, u32[]{:S(2)}) copy-start(f32[630,315]{0,1:T(8,128)} %param.10) | copy-start | bytes 2381404

commit v6 on v5

--- a/solution.py
+++ b/solution.py
@@ -12,7 +12,7 @@
 BF16 = jnp.bfloat16
 VMEM_LIMIT = 24 * 2**20
 SENDS = 40
-ROW_GROUPS = ((0, 256), (256, 512), (512, 640))
+ROW_GROUPS = ((0, 384), (384, 640))
 
 
 def two_parts(x):
@@ -114,36 +114,34 @@
             self.s1[g, h][0].wait_recv()
             self.total[g][self.a, h] += self.ins[0][g][h, 0]
 
+    def pair(self, h, i):
+        at = (i + 1) % 4 if h == 0 else i
+        return at - at % 2
+
     def step3(self, g):
         for h in range(2):
             p, _ = order(self.b, h)
             self.s2[g, h].wait_recv()
             self.total[g][self.a, h] += self.ins[1][g][h]
-            to = self.at(self.a, p)
-            self.s3[g, h] = [
-                self.exchange(self.total[g].at[self.a, h, i], self.ins[2][g].at[h, n], to)
-                for n, i in enumerate((p, far(self.b)))
-            ]
+            theirs = self.total[g].at[self.a, h, pl.ds(self.pair(h, p), 2)]
+            self.s3[g, h] = self.exchange(theirs, self.ins[2][g].at[h], self.at(self.a, p))
 
     def step4(self, g):
         for h in range(2):
-            p, q = order(self.b, h)
-            to = self.at(self.a, q)
-            for n, i in enumerate((self.b, q)):
-                self.s3[g, h][n].wait_recv()
-                self.total[g][self.a, h, i] += self.ins[2][g][h, n]
-            self.s4[g, h] = [
-                self.exchange(self.total[g].at[self.a, h, i], self.ins[3][g].at[h, 1 - n], to)
-                for n, i in enumerate((self.b, q))
-            ]
+            _, q = order(self.b, h)
+            mine = pl.ds(self.pair(h, self.b), 2)
+            self.s3[g, h].wait_recv()
+            self.total[g][self.a, h, mine] += self.ins[2][g][h]
+            self.s4[g, h] = self.exchange(
+                self.total[g].at[self.a, h, mine], self.ins[3][g].at[h], self.at(self.a, q)
+            )
 
     def blocks(self):
-        return [(h, i) for h in range(2) for i in (self.b, order(self.b, h)[1])]
+        return [(h, self.pair(h, self.b) + n) for h in range(2) for n in range(2)]
 
     def result(self, g):
         for h in range(2):
-            for copy in self.s4[g, h]:
-                copy.wait_recv()
+            self.s4[g, h].wait_recv()
         parts = [
             self.total[g][self.a, h, i] + self.ins[3][g][h, n % 2]
             for n, (h, i) in enumerate(self.blocks())
@@ -154,21 +152,14 @@
         for n, (h, i) in enumerate(self.blocks()):
             self.full[g][self.a, h, i] = value[8 * n : 8 * n + 8]
         for h in range(2):
-            p, q = order(self.b, h)
-            self.g1[g, h] = [
-                self.exchange(
-                    self.full[g].at[self.a, h, i],
-                    self.full[g].at[self.a, h, i],
-                    self.at(self.a, p),
-                )
-                for i in (self.b, q)
-            ]
+            p, _ = order(self.b, h)
+            mine = self.full[g].at[self.a, h, pl.ds(self.pair(h, self.b), 2)]
+            self.g1[g, h] = self.exchange(mine, mine, self.at(self.a, p))
 
     def gather2(self, g):
         for h in range(2):
             p, q = order(self.a, h)
-            for copy in self.g1[g, h]:
-                copy.wait_recv()
+            self.g1[g, h].wait_recv()
             own = self.full[g].at[self.a, h]
             self.g2[g, h] = self.exchange(own, own, self.at(q, self.b))
             self.g3[g, h] = [self.exchange(own, own, self.at(p, self.b))]
@@ -187,7 +178,7 @@
 
 
 def kernel(
-    al_in, w_in, j_ref, f_in, fm_in, fs_in, g_ref, field_ref,
+    al_in, w_in, j_ref, f_in, fm_in, fs_in, pm_in, ps_in, g_ref, field_ref, pm_ref, ps_ref,
     states, oc32, or32, oct, j_pad, j_high, j_low, j_in, xr, xc,
     r_in1, r_in2, r_in3, r_in4, c_in1, c_in2, c_in3, c_in4, wr, wc, acc,
     fpad, fg_ref, al_ref, w_ref, j_own, f_ref, fm_ref, fs_ref, local, state_send, send, recv,
@@ -208,7 +199,7 @@
     loads = [
         pltpu.make_async_copy(src, dst, local.at[n])
         for n, (src, dst) in enumerate(
-            ((al_in, al_ref), (f_in, f_ref), (j_ref, j_own), (w_in, w_ref), (fm_in, fm_ref), (fs_in, fs_ref))
+            ((al_in, al_ref), (f_in, f_ref), (j_ref, j_own), (w_in, w_ref), (fm_in, fm_ref), (fs_in, fs_ref), (pm_in, pm_ref), (ps_in, ps_ref))
         )
     ]
     for load in loads:
@@ -242,7 +233,7 @@
     words = jnp.where(word_line == 6, fields0, jnp.where(word_line == 7, fields1, words))
 
     loads[2].wait()
-    for load in loads[3:]:
+    for load in loads[3:6]:
         load.wait()
     j_pad[...] = jnp.zeros_like(j_pad)
     j_pad[0:315, 0:630] = j_own[...]
@@ -503,6 +494,8 @@
     grad = jnp.concatenate([natural_tile(grad_tile, t) for t in range(5)], axis=1)
     field_ref[3:4, :] = grad[0:1]
 
+    for load in loads[6:]:
+        load.wait()
     for copy in copies[-SENDS:]:
         copy.wait_send()
 
@@ -528,14 +521,15 @@
     def by_group(*dims):
         return [pltpu.VMEM((*dims, high - low), F32) for low, high in ROW_GROUPS]
 
-    sums, field_lines = pl.pallas_call(
+    sums, field_lines, held_mean, held_square = pl.pallas_call(
         kernel,
         out_shape=(
             jax.ShapeDtypeStruct(couplings.shape[::-1], F32),
             jax.ShapeDtypeStruct((4, 640), F32),
+            *[jax.ShapeDtypeStruct(couplings.shape[::-1], F32)] * 2,
         ),
-        in_specs=[pl.BlockSpec(memory_space=pltpu.HBM)] * 6,
-        out_specs=(vmem, vmem),
+        in_specs=[pl.BlockSpec(memory_space=pltpu.HBM)] * 8,
+        out_specs=(vmem,) * 4,
         scratch_shapes=[
             pltpu.VMEM((8, 512), F32),
             pltpu.VMEM((64, 8, 384), F32),
@@ -562,16 +556,20 @@
             pltpu.VMEM((1, 512), F32),
             pltpu.VMEM(couplings.shape[::-1], F32),
             *[pltpu.VMEM(fields.shape, F32)] * 3,
-            pltpu.SemaphoreType.DMA((6,)),
+            pltpu.SemaphoreType.DMA((8,)),
             pltpu.SemaphoreType.DMA((16,)),
             pltpu.SemaphoreType.DMA((SENDS,)),
-            pltpu.SemaphoreType.DMA((26 + 32 * len(ROW_GROUPS),)),
+            pltpu.SemaphoreType.DMA((20 + 26 * len(ROW_GROUPS),)),
         ],
         compiler_params=pltpu.CompilerParams(collective_id=0, has_side_effects=True, vmem_limit_bytes=VMEM_LIMIT),
     )(*(
         pltpu.with_memory_space_constraint(x, pltpu.HBM)
-        for x in (alignment.T, seq_weight.reshape(1, -1), couplings.T, fields, field_mean, field_square)
+        for x in (
+            alignment.T, seq_weight.reshape(1, -1), couplings.T,
+            fields, field_mean, field_square, pair_mean.T, pair_square.T,
+        )
     ))
+    pair_mean, pair_square = held_mean.T, held_square.T
     sums = sums.T
     row_residues = alignment.shape[1]
     column_residues = couplings.shape[1] // Q

time: 63.8 us -> 62.4 us (0.978)
  other arithmetic: 4.07 us -> 2.66 us
    sub x2, other arithmetic: 4.01 us -> 2.6 us  [adam_update(): return (values - change, first_new, second_new)]
where the time goes in v6:
time: 62.4 us; the launch traced here: 62.2 us
  Pallas kernels  58.9 us (94%)
  other arithmetic  2.66 us (4%)
  between operations  0.67 us (1%)
    pallas_call x1, Pallas kernels, on_device(): pl.pallas_call(kernel, out_shape=(jax.ShapeDtypeStruct(couplings.shape[::...  58.9 us
    sub x2, other arithmetic, adam_update(): return (values - change, first_new, second_new)  2.6 us

profile of v6, /device:TPU:1, one launch (start us, length us, event | category | flops | bytes accessed | tf_op | source)
XLA Modules:
  0.0 62.2 jit_solution(4770429040880817472)
XLA Ops:
  0.7 0.0 copy-start
  0.7 58.9 %shard_map.127 = (f32[315,630]{1,0:T(8,128)S(1)}, f32[4,640]{1,0:T(4,128)S(1)}, f32[315,630]{1,0:T(8,128)S(1)}, f32[315,630]{1,0:T(8,128)S(1)}) custom-call(s32[30,512]{1,0:T(8,128)} %bitcast.24, f32[1,512]{1,0:T(1,128)} %bitcast.25, f32[315,630]{1,0:T(8,128)} %bitcast.21, f32[630]{0:T(1024)} %f_in.1, f32[630]{0:T(1024)} %fm_in.1, f32[630]{0:T(1024)} %fs_in.1, ...), custom_call_target="tpu_custom_call" | custom-call | tf_op jit(solution)/shard_map/pallas_call | solution.py:524
  59.6 0.0 copy-done
  59.6 2.0 %divide_subtract_fusion = (f32[630,315]{0,1:T(8,128)}, f32[630,315]{0,1:T(8,128)}, f32[630,315]{0,1:T(8,128)}) fusion(f32[630,315]{0,1:T(8,128)S(1)} %copy-done, f32[315,630]{1,0:T(8,128)S(1)} %get-tuple-element.11, s32[315]{0:T(512)S(1)} %fusion.7, s32[630]{0:T(1024)S(1)} %fusion.2, f32[315,630]{1,0:T(8,128)S(1)} %get-tuple-element.10, ...), kind=kLoop, calls=%fused_computation.5 | loop fusion | flops 3175200 | bytes 5560380 | tf_op jit(solution)/shard_map/sub | solution.py:513
  61.6 0.6 divide_subtract_fusion.1
  (3 shorter events, 0.1 us)
Async XLA Ops:
  0.7 58.9 %copy-start = (f32[630,315]{0,1:T(8,128)S(1)}, f32[630,315]{0,1:T(8,128)}, u32[]{:S(2)}) copy-start(f32[630,315]{0,1:T(8,128)} %param.10) | copy-start | bytes 2381404

commit v7 on v6

--- a/solution.py
+++ b/solution.py
@@ -257,36 +257,6 @@
     or32[...] = hot_r.reshape(64, 8, 640)
     hot_r = hot_r.astype(BF16)
 
-    pl.semaphore_wait(barrier, len(greeted))
-
-    state_copies = [
-        pltpu.make_async_remote_copy(
-            states, states, state_send.at[d], recv.at[0],
-            device_id=((row + d) % 16, col), device_id_type=MESH,
-        )
-        for d in range(1, 16)
-    ]
-
-    @pl.when(row == owner)
-    def _():
-        states[...] = words
-        for copy in state_copies:
-            copy.start()
-
-    copies = []
-
-    def exchange(src, dst, device):
-        at = len(copies)
-        if at >= SENDS:
-            copies[at - SENDS].wait_send()
-        copy = pltpu.make_async_remote_copy(
-            src, dst, send.at[at % SENDS], recv.at[at + 1], device_id=device, device_id_type=MESH
-        )
-        copy.start()
-        copies.append(copy)
-        return copy
-
-    across = exchange(j_ref, j_in, partner)
     nt = ((1,), (1,))
     top, bottom = hot_r[0:256], hot_r[256:512]
     none = jnp.zeros((64, 640), BF16)
@@ -300,6 +270,36 @@
         sum(dot(top, j, nt) for j in tails1) + sum(dot(bottom, j, nt) for j in tails2)
     ).reshape(4, 2, 4, 8, 128)
 
+    pl.semaphore_wait(barrier, len(greeted))
+
+    state_copies = [
+        pltpu.make_async_remote_copy(
+            states, states, state_send.at[d], recv.at[0],
+            device_id=((row + d) % 16, col), device_id_type=MESH,
+        )
+        for d in range(1, 16)
+    ]
+
+    @pl.when(row == owner)
+    def _():
+        states[...] = words
+        for copy in state_copies:
+            copy.start()
+
+    copies = []
+
+    def exchange(src, dst, device):
+        at = len(copies)
+        if at >= SENDS:
+            copies[at - SENDS].wait_send()
+        copy = pltpu.make_async_remote_copy(
+            src, dst, send.at[at % SENDS], recv.at[at + 1], device_id=device, device_id_type=MESH
+        )
+        copy.start()
+        copies.append(copy)
+        return copy
+
+    across = exchange(j_ref, j_in, partner)
     cols = Reduce(
         exchange, x, z_lo, at_col, [xc], ([c_in1], [c_in2], [c_in3], [c_in4]), [wc]
     )
@@ -354,6 +354,8 @@
         sums = dot(hot_b, j_high[:, at]) + dot(hot_b, j_low[:, at])
         xr[g][...] = sums.reshape(4, 2, 4, 8, -1)
         rows.step1(g)
+
+    cols.step2(0)
 
     lane_c = iota((1, 384), 1)
     spread_c = digit_residue((40, 384), 0) == core * 15 + residue_of(iota((40, 384), 1))
@@ -368,16 +370,12 @@
     oct[0] = hot_t[:, 0:256]
     oct[1] = hot_t[:, 256:512]
 
-    cols.step2(0)
+    cols.step3(0)
     for g in row_groups:
         rows.step2(g)
-    cols.step3(0)
+    cols.step4(0)
     for g in row_groups:
         rows.step3(g)
-    cols.step4(0)
-
-    for g in row_groups:
-        rows.step4(g)
 
     def line_weights(first):
         lane = iota((8, 512), 1) - iota((8, 512), 0)
@@ -414,6 +412,9 @@
     fields_c = jnp.concatenate([f_main, f_main, f_tail], axis=1)
     weight = jnp.where(second, line_weights(first + 256), line_weights(first))
     cols.gather1(0, residual(cols.result(0) + fields_c, hot, residue_c, weight))
+    for g in row_groups:
+        rows.step4(g)
+    cols.gather2(0)
 
     block = core * 32 + y * 8
     first_blocks = rows.blocks()
@@ -425,8 +426,6 @@
         hot = jnp.concatenate([or32[block + 4 * h + i, :, at] for h, i in rows.blocks()], axis=0)
         energy = rows.result(g) + fields_r[:, low:high]
         rows.gather1(g, residual(energy, hot, res_r[:, low:high], weight))
-        if g == 0:
-            cols.gather2(0)
     cols.gather3(0)
     for g in row_groups:
         rows.gather2(g)

time: 62.4 us -> 64.8 us (1.038)
  Pallas kernels: 58.9 us -> 61.3 us
    pallas_call x1, Pallas kernels: 58.9 us -> 61.3 us  [on_device(): pl.pallas_call(kernel, out_shape=(jax.ShapeDtypeStruct(couplings.shape[::...]
where the time goes in v7:
time: 64.8 us; the launch traced here: 64.7 us
  Pallas kernels  61.3 us (95%)
  other arithmetic  2.66 us (4%)
  between operations  0.67 us (1%)
    pallas_call x1, Pallas kernels, on_device(): pl.pallas_call(kernel, out_shape=(jax.ShapeDtypeStruct(couplings.shape[::...  61.3 us
    sub x2, other arithmetic, adam_update(): return (values - change, first_new, second_new)  2.6 us

profile of v7, /device:TPU:1, one launch (start us, length us, event | category | flops | bytes accessed | tf_op | source)
XLA Modules:
  0.0 64.7 jit_solution(2435415248768792488)
XLA Ops:
  0.7 0.0 copy-start
  0.7 61.3 %shard_map.127 = (f32[315,630]{1,0:T(8,128)S(1)}, f32[4,640]{1,0:T(4,128)S(1)}, f32[315,630]{1,0:T(8,128)S(1)}, f32[315,630]{1,0:T(8,128)S(1)}) custom-call(s32[30,512]{1,0:T(8,128)} %bitcast.24, f32[1,512]{1,0:T(1,128)} %bitcast.25, f32[315,630]{1,0:T(8,128)} %bitcast.21, f32[630]{0:T(1024)} %f_in.1, f32[630]{0:T(1024)} %fm_in.1, f32[630]{0:T(1024)} %fs_in.1, ...), custom_call_target="tpu_custom_call" | custom-call | tf_op jit(solution)/shard_map/pallas_call | solution.py:523
  62.0 0.0 copy-done
  62.0 2.0 %divide_subtract_fusion = (f32[630,315]{0,1:T(8,128)}, f32[630,315]{0,1:T(8,128)}, f32[630,315]{0,1:T(8,128)}) fusion(f32[630,315]{0,1:T(8,128)S(1)} %copy-done, f32[315,630]{1,0:T(8,128)S(1)} %get-tuple-element.11, s32[315]{0:T(512)S(1)} %fusion.7, s32[630]{0:T(1024)S(1)} %fusion.2, f32[315,630]{1,0:T(8,128)S(1)} %get-tuple-element.10, ...), kind=kLoop, calls=%fused_computation.5 | loop fusion | flops 3175200 | bytes 5560380 | tf_op jit(solution)/shard_map/sub | solution.py:512
  64.1 0.6 divide_subtract_fusion.1
  (3 shorter events, 0.1 us)
Async XLA Ops:
  0.7 61.4 %copy-start = (f32[630,315]{0,1:T(8,128)S(1)}, f32[630,315]{0,1:T(8,128)}, u32[]{:S(2)}) copy-start(f32[630,315]{0,1:T(8,128)} %param.10) | copy-start | bytes 2381404

commit v8 on v6

--- a/solution.py
+++ b/solution.py
@@ -374,10 +374,9 @@
     cols.step3(0)
     for g in row_groups:
         rows.step3(g)
+    for g in row_groups:
+        rows.step4(g)
     cols.step4(0)
-
-    for g in row_groups:
-        rows.step4(g)
 
     def line_weights(first):
         lane = iota((8, 512), 1) - iota((8, 512), 0)
@@ -425,8 +424,7 @@
         hot = jnp.concatenate([or32[block + 4 * h + i, :, at] for h, i in rows.blocks()], axis=0)
         energy = rows.result(g) + fields_r[:, low:high]
         rows.gather1(g, residual(energy, hot, res_r[:, low:high], weight))
-        if g == 0:
-            cols.gather2(0)
+    cols.gather2(0)
     cols.gather3(0)
     for g in row_groups:
         rows.gather2(g)

time: 62.4 us -> 66.1 us (1.059)
  Pallas kernels: 58.9 us -> 62.6 us
    pallas_call x1, Pallas kernels: 58.9 us -> 62.6 us  [on_device(): pl.pallas_call(kernel, out_shape=(jax.ShapeDtypeStruct(couplings.shape[::...]
where the time goes in v8:
time: 66.1 us; the launch traced here: 65.9 us
  Pallas kernels  62.6 us (95%)
  other arithmetic  2.66 us (4%)
  between operations  0.67 us (1%)
    pallas_call x1, Pallas kernels, on_device(): pl.pallas_call(kernel, out_shape=(jax.ShapeDtypeStruct(couplings.shape[::...  62.6 us
    sub x2, other arithmetic, adam_update(): return (values - change, first_new, second_new)  2.6 us

profile of v8, /device:TPU:1, one launch (start us, length us, event | category | flops | bytes accessed | tf_op | source)
XLA Modules:
  0.0 65.9 jit_solution(3469041013340582781)
XLA Ops:
  0.7 0.0 copy-start
  0.7 62.6 %shard_map.127 = (f32[315,630]{1,0:T(8,128)S(1)}, f32[4,640]{1,0:T(4,128)S(1)}, f32[315,630]{1,0:T(8,128)S(1)}, f32[315,630]{1,0:T(8,128)S(1)}) custom-call(s32[30,512]{1,0:T(8,128)} %bitcast.24, f32[1,512]{1,0:T(1,128)} %bitcast.25, f32[315,630]{1,0:T(8,128)} %bitcast.21, f32[630]{0:T(1024)} %f_in.1, f32[630]{0:T(1024)} %fm_in.1, f32[630]{0:T(1024)} %fs_in.1, ...), custom_call_target="tpu_custom_call" | custom-call | tf_op jit(solution)/shard_map/pallas_call | solution.py:522
  63.3 0.0 copy-done
  63.3 2.0 %divide_subtract_fusion = (f32[630,315]{0,1:T(8,128)}, f32[630,315]{0,1:T(8,128)}, f32[630,315]{0,1:T(8,128)}) fusion(f32[630,315]{0,1:T(8,128)S(1)} %copy-done, f32[315,630]{1,0:T(8,128)S(1)} %get-tuple-element.11, s32[315]{0:T(512)S(1)} %fusion.7, s32[630]{0:T(1024)S(1)} %fusion.2, f32[315,630]{1,0:T(8,128)S(1)} %get-tuple-element.10, ...), kind=kLoop, calls=%fused_computation.5 | loop fusion | flops 3175200 | bytes 5560380 | tf_op jit(solution)/shard_map/sub | solution.py:511
  65.3 0.6 divide_subtract_fusion.1
  (3 shorter events, 0.1 us)
Async XLA Ops:
  0.7 62.6 %copy-start = (f32[630,315]{0,1:T(8,128)S(1)}, f32[630,315]{0,1:T(8,128)}, u32[]{:S(2)}) copy-start(f32[630,315]{0,1:T(8,128)} %param.10) | copy-start | bytes 2381404
